TPU v7x, 768 devices: a whole 4x8x12 slice. The times are simulated.
768 devices in a mesh: mem: 32 (over y, x_hi, core), lat: 24 (over x_lo, z).
Axes of the slice: x: 4 (x_hi: 2, x_lo: 2; x = x_hi * 2 + x_lo), y: 8, z: 12, core: 2. Of those that a mesh axis runs over, the one named last changes fastest.
Arguments:
- ensemble: float32 [256, 4, 96, 1024], P('mem', None, 'lat'), may hold values from -6 to 6
- obs_value: float32 [1, 768, 16], P(None, ('mem', 'lat')), may hold values from -9 to 9
- obs_var: float32 [1, 768, 16], P(None, ('mem', 'lat')), may hold values from 0.5 to 4
- obs_cell: int32 [1, 768, 16], P(None, ('mem', 'lat')), may hold values from 0 to 511
- obs_loop: int32 [1, 768, 16], P(None, ('mem', 'lat')), may hold values from 0 to 3
- obs_count: int32 [1, 768], P(None, ('mem', 'lat')), may hold values from 8 to 16, as said below
Outputs:
- analysis: float32 [256, 4, 96, 1024], P('mem', None, 'lat')
Inputs may be any that keep to these rules, and one draw needn't show every extreme that they name: `obs_count`: at least 8 and at most 16 slots live per patch; in each cycle some patch has all 16 slots live and another exactly 8.
All inputs are finite; a program needn't handle non-finite values.
Results may differ from a plain program's by a relative error of at most 0.0003.
Values sent between devices are 32-bit elements; how exact they have to be, the bound alone decides.
A program may use at most 32 MiB of HBM per device.

v0:
```python
import jax
import jax.numpy as jnp
from jax import lax
from jax.sharding import PartitionSpec as P

NSI = 5


time_step = 0.15
viscosity = 0.1
third_part = 1.0 / 3.0
two_thirds = 2.0 / 3.0


def with_halo(cells, sides, width):
    for axis, dim in sides:
        count = lax.axis_size(axis)
        ends = count - 1
        head = lax.slice_in_dim(cells, 0, width, axis=dim)
        tail = lax.slice_in_dim(cells, cells.shape[dim] - width, cells.shape[dim], axis=dim)
        cells = jnp.concatenate(
            [
                lax.ppermute(tail, axis, [(i, (i + 1) % count) for i in range(ends)]),
                cells,
                lax.ppermute(head, axis, [((i + 1) % count, i) for i in range(ends)]),
            ],
            axis=dim,
        )
    return cells


def tendency(padded):
    centre = padded[:, :, 1:-1, 1:-1]
    to_north = padded[:, :, 2:, 1:-1]
    to_south = padded[:, :, :-2, 1:-1]
    to_east = padded[:, :, 1:-1, 2:]
    to_west = padded[:, :, 1:-1, :-2]
    zonal_wind = centre[:, 0:1]
    meridional = centre[:, 1:2]
    moved = zonal_wind * (to_east - to_west) * 0.5 + meridional * (to_north - to_south) * 0.5
    return -moved + viscosity * (to_north + to_south + to_east + to_west - 4.0 * centre)


def widen(state, width):
    widened = with_halo(state, (("lat", 2),), width)
    return jnp.concatenate([widened[..., -width:], widened, widened[..., :width]], axis=3)


def advance_single(state):
    first = state + time_step * tendency(widen(state, 1))
    second = 0.75 * state + 0.25 * (first + time_step * tendency(widen(first, 1)))
    return third_part * state + two_thirds * (second + time_step * tendency(widen(second, 1)))


def analyse(cells, values, variance, slot_cell, slot_loop, count):
    members = cells.shape[0]
    highest = lax.Precision.HIGHEST
    centre_mean = jnp.mean(cells, axis=0)
    perturb = cells - centre_mean
    seen = jnp.take(cells, slot_cell, axis=1)
    seen_mean = jnp.mean(seen, axis=0)
    seen_pert = seen - seen_mean
    slots = jnp.arange(slot_cell.shape[0], dtype=jnp.int32)
    weight = jnp.where(
        slots < count, jnp.exp(-0.35 * slot_loop.astype(cells.dtype)) / variance, 0.0
    )
    scaled = seen_pert * weight
    gram = jnp.dot(scaled, seen_pert.T, precision=highest)
    drive = jnp.dot(scaled, values - seen_mean, precision=highest)
    identity = jnp.eye(members, dtype=cells.dtype)
    bound = members - 1.0 + 0.5 * jnp.trace(gram)
    root_up = ((members - 1.0) * identity + gram) / bound
    root_down = identity
    for repeat in range(NSI):
        factor = 1.5 * identity - 0.5 * jnp.dot(root_down, root_up, precision=highest)
        root_up = jnp.dot(root_up, factor, precision=highest)
        root_down = jnp.dot(factor, root_down, precision=highest)
    spread = root_down * jnp.sqrt((members - 1.0) / bound)
    centre_shift = (
        jnp.dot(root_down, jnp.dot(root_down, drive, precision=highest), precision=highest) / bound
    )
    transform = spread + centre_shift[:, None]
    return centre_mean + jnp.dot(transform.T, perturb, precision=highest)


def per_device(ensemble, obs_value, obs_var, obs_cell, obs_loop, obs_count):
    state = ensemble
    state = advance_single(state)
    state = lax.all_to_all(state, "mem", split_axis=3, concat_axis=0, tiled=True)
    members, fields, band_rows, lon_part = state.shape
    cells = state.reshape(members, fields * band_rows * lon_part)
    updated = analyse(
        cells, obs_value[0, 0], obs_var[0, 0], obs_cell[0, 0], obs_loop[0, 0], obs_count[0, 0]
    )
    state = updated.reshape(members, fields, band_rows, lon_part)
    state = lax.all_to_all(state, "mem", split_axis=0, concat_axis=3, tiled=True)
    return state


def solution(mesh):
    placed = (
        P("mem", None, "lat", None),
        P(None, ("mem", "lat"), None),
        P(None, ("mem", "lat"), None),
        P(None, ("mem", "lat"), None),
        P(None, ("mem", "lat"), None),
        P(None, ("mem", "lat")),
    )
    return jax.shard_map(
        per_device,
        mesh=mesh,
        in_specs=placed,
        out_specs=P("mem", None, "lat", None),
        check_vma=False,
    )
```

profile of v0, /device:TPU:6, one launch (start us, length us, event | category | flops | bytes accessed | tf_op | source)
XLA Modules:
  0.0 155.4 jit_solution(12220231877902158805)
XLA Ops:
  0.0 1.4 copy.53
  1.5 4.3 %collective-permute-start = (f32[8,4,1,1024]{3,0,2,1:T(8,128)S(1)}, f32[8,4,1,1024]{3,0,2,1:T(8,128)S(1)}, u32[]{:S(2)}, u32[]{:S(2)}) collective-permute-start(f32[8,4,1,1024]{3,0,2,1:T(8,128)S(1)} %get-tuple-element.17), channel_id=1, source_target_pairs={{0,1},{1,2},{2,3},{3,4},{4,5},{5,6},{6,7},{7,8},{8,9},{9,10},{10,1... | collective-permute-start | bytes 393224 | tf_op jit(solution)/shard_map/ppermute | solution.py:23
  5.7 12.5 %collective-permute-start.1 = (f32[8,4,1,1024]{3,0,2,1:T(8,128)S(1)}, f32[8,4,1,1024]{3,0,2,1:T(8,128)S(1)}, u32[]{:S(2)}, u32[]{:S(2)}) collective-permute-start(f32[8,4,1,1024]{3,0,2,1:T(8,128)S(1)} %get-tuple-element.18), channel_id=1, source_target_pairs={{1,0},{2,1},{3,2},{4,3},{5,4},{6,5},{7,6},{8,7},{9,8},{10,9},{11,1... | collective-permute-start | bytes 393224 | tf_op jit(solution)/shard_map/ppermute | solution.py:25
  18.2 1.0 slice_bitcast_fusion.5
  19.4 0.4 collective-permute-done
  20.1 0.8 collective-permute-done.1
  21.1 0.5 multiply_add_fusion.2
  21.6 1.9 %collective-permute-start.2 = (f32[8,4,1,1024]{3,0,2,1:T(8,128)S(1)}, f32[8,4,1,1024]{3,0,2,1:T(8,128)S(1)}, u32[]{:S(2)}, u32[]{:S(2)}) collective-permute-start(f32[8,4,1,1024]{3,0,2,1:T(8,128)S(1)} %get-tuple-element.13), channel_id=1, source_target_pairs={{0,1},{1,2},{2,3},{3,4},{4,5},{5,6},{6,7},{7,8},{8,9},{9,10},{10,1... | collective-permute-start | bytes 393224 | tf_op jit(solution)/shard_map/ppermute | solution.py:23
  23.5 6.5 %collective-permute-start.3 = (f32[8,4,1,1024]{3,0,2,1:T(8,128)S(1)}, f32[8,4,1,1024]{3,0,2,1:T(8,128)S(1)}, u32[]{:S(2)}, u32[]{:S(2)}) collective-permute-start(f32[8,4,1,1024]{3,0,2,1:T(8,128)S(1)} %get-tuple-element.14), channel_id=1, source_target_pairs={{1,0},{2,1},{3,2},{4,3},{5,4},{6,5},{7,6},{8,7},{9,8},{10,9},{11,1... | collective-permute-start | bytes 393224 | tf_op jit(solution)/shard_map/ppermute | solution.py:25
  30.1 1.0 collective-permute-done.2
  31.0 1.5 collective-permute-done.3
  32.5 0.6 multiply_add_fusion.1
  33.2 1.9 %collective-permute-start.4 = (f32[8,4,1,1024]{3,0,2,1:T(8,128)S(1)}, f32[8,4,1,1024]{3,0,2,1:T(8,128)S(1)}, u32[]{:S(2)}, u32[]{:S(2)}) collective-permute-start(f32[8,4,1,1024]{3,0,2,1:T(8,128)S(1)} %get-tuple-element.9), channel_id=1, source_target_pairs={{0,1},{1,2},{2,3},{3,4},{4,5},{5,6},{6,7},{7,8},{8,9},{9,10},{10,1... | collective-permute-start | bytes 393224 | tf_op jit(solution)/shard_map/ppermute | solution.py:23
  35.1 6.5 %collective-permute-start.5 = (f32[8,4,1,1024]{3,0,2,1:T(8,128)S(1)}, f32[8,4,1,1024]{3,0,2,1:T(8,128)S(1)}, u32[]{:S(2)}, u32[]{:S(2)}) collective-permute-start(f32[8,4,1,1024]{3,0,2,1:T(8,128)S(1)} %get-tuple-element.10), channel_id=1, source_target_pairs={{1,0},{2,1},{3,2},{4,3},{5,4},{6,5},{7,6},{8,7},{9,8},{10,9},{11,1... | collective-permute-start | bytes 393224 | tf_op jit(solution)/shard_map/ppermute | solution.py:25
  41.6 1.0 collective-permute-done.4
  42.6 1.5 collective-permute-done.5
  44.1 0.6 multiply_add_fusion
  44.7 6.1 %copy.64 = f32[8,4,4,1024]{0,2,1,3:T(4,128)} copy(f32[8,4,4,1024]{3,0,2,1:T(8,128)S(1)} %multiply_add_fusion) | data formatting | bytes 1048576 | tf_op jit(solution)/shard_map/add | solution.py:52
  50.8 12.1 %reshape.93 = f32[32,1,4096]{2,1,0:T(1,128)} reshape(f32[1024,4,4,8]{3,2,1,0:T(4,128)} %bitcast.82) | data formatting | bytes 1048576
  62.9 10.2 %all-to-all-start = ((f32[32,1,4096]{2,1,0:T(1,128)}), f32[32,1,4096]{2,1,0:T(1,128)S(1)}, u32[]{:S(2)}, u32[]{:S(2)}) async-start(f32[32,1,4096]{2,1,0:T(1,128)} %reshape.93), calls=%async_computation | async-start | bytes 1048576 | tf_op jit(solution)/shard_map/all_to_all | solution.py:89
  73.9 17.0 %all-to-all-done = f32[32,1,4096]{2,1,0:T(1,128)S(1)} async-done(((f32[32,1,4096]{2,1,0:T(1,128)}), f32[32,1,4096]{2,1,0:T(1,128)S(1)}, u32[]{:S(2)}, u32[]{:S(2)}) %all-to-all-start) | async-done | bytes 524320 | tf_op jit(solution)/shard_map/all_to_all | solution.py:89
  90.8 0.5 broadcast.192
  91.3 1.9 %reduce.2 = f32[32,4096]{1,0:T(8,128)S(1)} reduce(f32[32,1,4096]{2,1,0:T(1,128)S(1)} %all-to-all-done, f32[]{:T(128)} %broadcast.192), dimensions={1}, to_apply=%all_to_all.24.reduce_sub_computation | reduce | bytes 1048580 | tf_op jit(solution)/shard_map/all_to_all | solution.py:89
  93.2 11.3 %reshape.94 = f32[1024,4,4,8]{3,2,1,0:T(4,128)} reshape(f32[32,4096]{1,0:T(8,128)S(1)} %reduce.2) | data formatting | bytes 1048576
  104.6 7.6 %copy.65 = f32[8,4,4,32,32]{4,2,1,0,3:T(4,128)S(1)} copy(f32[8,4,4,32,32]{0,2,1,4,3:T(4,128)} %bitcast.81) | data formatting | bytes 1048576 | tf_op jit(solution)/shard_map/all_to_all | solution.py:89
  112.2 1.9 %reshape.76 = f32[256,512]{1,0:T(8,128)S(1)} reshape(f32[32,8,4,4,32]{4,3,2,1,0:T(4,128)S(1)} %bitcast.83) | data formatting | bytes 1048576 | tf_op jit(solution)/shard_map/reshape | solution.py:91
  114.3 0.6 gather_fusion
  115.1 1.1 select_reduce_fusion
  117.1 0.4 fusion.16
  117.8 0.4 fusion.3
  118.6 0.4 fusion.43
  118.9 0.4 fusion.2
  119.3 0.4 fusion.46
  120.1 0.4 fusion.1
  120.5 0.4 fusion.48
  120.9 0.4 fusion.47
  121.3 0.4 bitcast_reduce_fusion
  121.9 0.4 fusion
  122.3 0.4 fusion.49
  123.5 0.7 convolution_add_fusion
  124.4 1.3 copy.68
  125.8 1.4 reshape.95
  127.1 22.5 %all_to_all.33 = f32[32,1,4096]{2,1,0:T(1,128)S(1)} all-to-all(f32[32,1,4096]{2,1,0:T(1,128)S(1)} %reshape.95), channel_id=1, replica_groups=mesh['mem'=32,'lat'=24] {'mem'}, dimensions={0} | all-to-all | bytes 1048576 | tf_op jit(solution)/shard_map/all_to_all | solution.py:96
  149.6 1.9 %reduce.3 = f32[32,4096]{1,0:T(8,128)S(1)} reduce(f32[32,1,4096]{2,1,0:T(1,128)S(1)} %all_to_all.33, f32[]{:T(128)} %broadcast.192), dimensions={1}, to_apply=%all_to_all.27.reduce_sub_computation | reduce | bytes 1048580 | tf_op jit(solution)/shard_map/all_to_all | solution.py:96
  151.5 1.1 reshape.96
  152.6 0.7 copy.78
  153.3 0.4 copy.72
  153.7 1.7 %reshape.92 = f32[8,4,4,1024]{3,2,1,0:T(4,128)} reshape(f32[8,4,4,32,32]{4,3,2,1,0:T(8,128)S(1)} %copy.72) | data formatting | bytes 1048576 | tf_op jit(solution)/shard_map/all_to_all | solution.py:96
  (38 shorter events, 3.6 us)
Async XLA Ops:
  0.0 19.8 %copy-start = (f32[8,4,4,1024]{3,2,1,0:T(4,128)S(1)}, f32[8,4,4,1024]{3,2,1,0:T(4,128)}, u32[]{:S(2)}) copy-start(f32[8,4,4,1024]{3,2,1,0:T(4,128)} %param.6) | copy-start | bytes 1572868
  1.5 18.3 %collective-permute-start = (f32[8,4,1,1024]{3,0,2,1:T(8,128)S(1)}, f32[8,4,1,1024]{3,0,2,1:T(8,128)S(1)}, u32[]{:S(2)}, u32[]{:S(2)}) collective-permute-start(f32[8,4,1,1024]{3,0,2,1:T(8,128)S(1)} %get-tuple-element.17), channel_id=1, source_target_pairs={{0,1},{1,2},{2,3},{3,4},{4,5},{5,6},{6,7},{7,8},{8,9},{9,10},{10,1... | collective-permute-start | bytes 393224 | tf_op jit(solution)/shard_map/ppermute | solution.py:23
  5.7 15.2 %collective-permute-start.1 = (f32[8,4,1,1024]{3,0,2,1:T(8,128)S(1)}, f32[8,4,1,1024]{3,0,2,1:T(8,128)S(1)}, u32[]{:S(2)}, u32[]{:S(2)}) collective-permute-start(f32[8,4,1,1024]{3,0,2,1:T(8,128)S(1)} %get-tuple-element.18), channel_id=1, source_target_pairs={{1,0},{2,1},{3,2},{4,3},{5,4},{6,5},{7,6},{8,7},{9,8},{10,9},{11,1... | collective-permute-start | bytes 393224 | tf_op jit(solution)/shard_map/ppermute | solution.py:25
  21.6 9.4 %collective-permute-start.2 = (f32[8,4,1,1024]{3,0,2,1:T(8,128)S(1)}, f32[8,4,1,1024]{3,0,2,1:T(8,128)S(1)}, u32[]{:S(2)}, u32[]{:S(2)}) collective-permute-start(f32[8,4,1,1024]{3,0,2,1:T(8,128)S(1)} %get-tuple-element.13), channel_id=1, source_target_pairs={{0,1},{1,2},{2,3},{3,4},{4,5},{5,6},{6,7},{7,8},{8,9},{9,10},{10,1... | collective-permute-start | bytes 393224 | tf_op jit(solution)/shard_map/ppermute | solution.py:23
  23.5 9.0 %collective-permute-start.3 = (f32[8,4,1,1024]{3,0,2,1:T(8,128)S(1)}, f32[8,4,1,1024]{3,0,2,1:T(8,128)S(1)}, u32[]{:S(2)}, u32[]{:S(2)}) collective-permute-start(f32[8,4,1,1024]{3,0,2,1:T(8,128)S(1)} %get-tuple-element.14), channel_id=1, source_target_pairs={{1,0},{2,1},{3,2},{4,3},{5,4},{6,5},{7,6},{8,7},{9,8},{10,9},{11,1... | collective-permute-start | bytes 393224 | tf_op jit(solution)/shard_map/ppermute | solution.py:25
  33.2 9.4 %collective-permute-start.4 = (f32[8,4,1,1024]{3,0,2,1:T(8,128)S(1)}, f32[8,4,1,1024]{3,0,2,1:T(8,128)S(1)}, u32[]{:S(2)}, u32[]{:S(2)}) collective-permute-start(f32[8,4,1,1024]{3,0,2,1:T(8,128)S(1)} %get-tuple-element.9), channel_id=1, source_target_pairs={{0,1},{1,2},{2,3},{3,4},{4,5},{5,6},{6,7},{7,8},{8,9},{9,10},{10,1... | collective-permute-start | bytes 393224 | tf_op jit(solution)/shard_map/ppermute | solution.py:23
  35.1 9.0 %collective-permute-start.5 = (f32[8,4,1,1024]{3,0,2,1:T(8,128)S(1)}, f32[8,4,1,1024]{3,0,2,1:T(8,128)S(1)}, u32[]{:S(2)}, u32[]{:S(2)}) collective-permute-start(f32[8,4,1,1024]{3,0,2,1:T(8,128)S(1)} %get-tuple-element.10), channel_id=1, source_target_pairs={{1,0},{2,1},{3,2},{4,3},{5,4},{6,5},{7,6},{8,7},{9,8},{10,9},{11,1... | collective-permute-start | bytes 393224 | tf_op jit(solution)/shard_map/ppermute | solution.py:25
  50.8 23.0 %copy-start.3 = (s32[1,1,16]{2,1,0:T(1,128)S(1)}, s32[1,1,16]{2,1,0:T(1,128)}, u32[]{:S(2)}) copy-start(s32[1,1,16]{2,1,0:T(1,128)} %param.9) | copy-start | bytes 196
  62.9 27.9 %all-to-all-start = ((f32[32,1,4096]{2,1,0:T(1,128)}), f32[32,1,4096]{2,1,0:T(1,128)S(1)}, u32[]{:S(2)}, u32[]{:S(2)}) async-start(f32[32,1,4096]{2,1,0:T(1,128)} %reshape.93), calls=%async_computation | async-start | bytes 1048576 | tf_op jit(solution)/shard_map/all_to_all | solution.py:89
  112.2 2.9 %copy-start.1 = (f32[1,1,16]{2,1,0:T(1,128)S(1)}, f32[1,1,16]{2,1,0:T(1,128)}, u32[]{:S(2)}) copy-start(f32[1,1,16]{2,1,0:T(1,128)} %param.8) | copy-start | bytes 196
  112.2 2.9 %copy-start.2 = (s32[1,1,16]{2,1,0:T(1,128)S(1)}, s32[1,1,16]{2,1,0:T(1,128)}, u32[]{:S(2)}) copy-start(s32[1,1,16]{2,1,0:T(1,128)} %param.10) | copy-start | bytes 196
  120.1 1.6 %copy-start.4 = (f32[1,1,16]{2,1,0:T(1,128)S(1)}, f32[1,1,16]{2,1,0:T(1,128)}, u32[]{:S(2)}) copy-start(f32[1,1,16]{2,1,0:T(1,128)} %param.7) | copy-start | bytes 196
where the time goes:
time: 156 us; the launch traced here: 155 us
  local copies, waits for them, and re-layouts  50.2 us (32%)
  starting transfers between devices  43.8 us (28%)
  waiting for transfers between devices  23.1 us (15%)
  blocking collectives  22.5 us (14%)
  matrix products  7.76 us (5%)
  other arithmetic  6.19 us (4%)
  between operations  1.81 us (1%)
    unnamed x17, local copies, waits for them, and re-layouts  27.6 us
    ppermute x3, starting transfers between devices, with_halo(): lax.ppermute(head, axis, [((i + 1) % count, i) for i in range(ends)])  25.5 us
    all_to_all x1, blocking collectives, per_device(): lax.all_to_all(state, 'mem', split_axis=0, concat_axis=3, tiled=True)  22.5 us
    all_to_all x1, waiting for transfers between devices, per_device(): lax.all_to_all(state, 'mem', split_axis=3, concat_axis=0, tiled=True)  17 us
    all_to_all x1, starting transfers between devices, per_device(): lax.all_to_all(state, 'mem', split_axis=3, concat_axis=0, tiled=True)  10.2 us
    all_to_all x2, local copies, waits for them, and re-layouts, per_device(): lax.all_to_all(state, 'mem', split_axis=3, concat_axis=0, tiled=True)  8.15 us
    ppermute x3, starting transfers between devices, with_halo(): lax.ppermute(tail, axis, [(i, (i + 1) % count) for i in range(ends)])  8.12 us
    add x1, local copies, waits for them, and re-layouts, advance_single(): third_part * state  6.07 us
  transfers between devices with their start and end apart: 7, of which 7 were waited for; matrix products, arithmetic and copies ran while one was open for 1% of the time, Pallas kernels for 0%

commit v1 on v0

v1 whole, which is shorter than its diff:
```python
import functools

import jax
import jax.numpy as jnp
from jax import lax
from jax.experimental import pallas as pl
from jax.experimental.pallas import tpu as pltpu
from jax.sharding import PartitionSpec as P

MESH = pl.DeviceIdType.MESH
NSI = 5
DT = 0.15
VISC = 0.1


def mm(a, b, dims=((1,), (0,))):
    return lax.dot_general(
        a, b, (dims, ((), ())), precision=lax.Precision.HIGHEST, preferred_element_type=jnp.float32
    )


def stage(source, base, target, rows, shift, weight_base, weight_mid):
    width = source.shape[-1]

    def row(i, _):
        u = source[i + 1, 0]
        v = source[i + 1, 1]
        scale = weight_mid * DT
        east_w = scale * VISC - (0.5 * scale) * u
        west_w = scale * VISC + (0.5 * scale) * u
        north_w = scale * VISC - (0.5 * scale) * v
        south_w = scale * VISC + (0.5 * scale) * v
        for f in range(4):
            c = source[i + 1, f]
            total = (weight_mid - 4.0 * scale * VISC) * c
            total += north_w * source[i + 2, f] + south_w * source[i, f]
            total += east_w * pltpu.roll(c, width - 1, 1) + west_w * pltpu.roll(c, 1, 1)
            if weight_base:
                total += weight_base * base[i + shift, f]
            target[i, f] = total
        return 0

    lax.fori_loop(0, rows, row, 0)


def analysis_weights(ypt, pert, onehot, xbar, values, variance, loop, count, members):
    nobs = ypt.shape[0]
    eye = (
        lax.broadcasted_iota(jnp.int32, (nobs, nobs), 0)
        == lax.broadcasted_iota(jnp.int32, (nobs, nobs), 1)
    )
    identity = jnp.where(eye, 1.0, 0.0)
    slots = lax.broadcasted_iota(jnp.int32, (1, nobs), 1)
    weight = jnp.where(slots < count, jnp.exp(-0.35 * loop) / variance, 0.0)

    def column(row):
        return jnp.sum(jnp.where(eye, row, 0.0), axis=1, keepdims=True)

    weight_col = column(weight)
    seen_mean = jnp.sum(onehot * xbar, axis=1, keepdims=True)
    innovation = column(values) - seen_mean
    cross = mm(ypt, pert)
    gram = mm(ypt, ypt, ((1,), (1,)))
    trace = jnp.sum(jnp.where(eye, gram * weight, 0.0), axis=(0, 1), keepdims=True)
    bound = members - 1.0 + 0.5 * trace
    a = (members - 1.0) / bound
    t = gram * weight / bound
    p0, p_m, p_h = a, a * identity + t, identity
    z0, z_m, z_h = jnp.ones_like(a), identity, jnp.zeros_like(identity)
    for repeat in range(NSI):
        g0 = 1.5 - 0.5 * p0
        g_m = 1.5 * identity - 0.5 * p_m
        g_h = -0.5 * p_h
        if repeat == 0:
            z_m, z_h, z0 = g_m, g_h, g0
            pg_m = mm(p_m, g_m)
            pg_h = g_m + p0 * g_h
        else:
            prod = mm(jnp.concatenate([p_m, p_h, z_m, z_h], axis=0), g_m)
            pg_m = prod[0:nobs]
            pg_h = prod[nobs : 2 * nobs] + p0 * g_h
            z_m = prod[2 * nobs : 3 * nobs]
            z_h = prod[3 * nobs :] + z0 * g_h
            z0 = z0 * g0
        if repeat < NSI - 1:
            prod = mm(jnp.concatenate([pg_m, pg_h], axis=0), g_m)
            p_m = prod[0:nobs]
            p_h = prod[nobs:] + (p0 * g0) * g_h
            p0 = p0 * g0 * g0
    spread = jnp.sqrt(a)
    step = mm(z_m, mm(z_m, innovation))
    shift_row = jnp.sum(weight_col * step * cross, axis=0, keepdims=True) / bound
    rows = mm((spread / bound) * weight_col * z_h, cross)
    return spread * z0, rows, xbar + shift_row


def kernel(
    x_ref, values_ref, variance_ref, cell_ref, loop_ref, count_ref, o_ref,
    wide, mid, mid2, last, packed, gathered, fresh, back,
    halo_send, halo_recv, send_a, recv_a, send_b, recv_b,
):
    n_mem, n_lat = lax.axis_size("mem"), lax.axis_size("lat")
    me, band = lax.axis_index("mem"), lax.axis_index("lat")
    north, south = lax.rem(band + 1, n_lat), lax.rem(band + n_lat - 1, n_lat)
    members, fields, rows, width = x_ref.shape
    group = n_mem // 8

    barrier = pltpu.get_barrier_semaphore()

    def greet(k, _):
        pl.semaphore_signal(
            barrier, inc=1, device_id={"mem": lax.rem(me + k, n_mem)}, device_id_type=MESH
        )
        return 0

    pl.semaphore_signal(barrier, inc=1, device_id={"lat": north}, device_id_type=MESH)
    pl.semaphore_signal(barrier, inc=1, device_id={"lat": south}, device_id_type=MESH)
    lax.fori_loop(1, n_mem, greet, 0)

    for r in range(rows):
        for f in range(fields):
            wide[3 + r, f] = x_ref[:, f, r, :]

    pl.semaphore_wait(barrier, n_mem + 1)

    upward = pltpu.make_async_remote_copy(
        src_ref=wide.at[pl.ds(rows, 3)], dst_ref=wide.at[pl.ds(0, 3)],
        send_sem=halo_send.at[0], recv_sem=halo_recv.at[0],
        device_id={"lat": north}, device_id_type=MESH,
    )
    downward = pltpu.make_async_remote_copy(
        src_ref=wide.at[pl.ds(3, 3)], dst_ref=wide.at[pl.ds(3 + rows, 3)],
        send_sem=halo_send.at[1], recv_sem=halo_recv.at[1],
        device_id={"lat": south}, device_id_type=MESH,
    )
    upward.start()
    downward.start()
    upward.wait()
    downward.wait()

    def clear(ref, start, size):
        ref[pl.ds(start, size)] = jnp.zeros((size,) + ref.shape[1:], ref.dtype)

    def clear_outside(ref, extra):
        @pl.when(band == 0)
        def _():
            clear(ref, 0, extra)

        @pl.when(band == n_lat - 1)
        def _():
            clear(ref, extra + rows, extra)

    clear_outside(wide, 3)
    stage(wide, None, mid, rows + 4, 0, 0.0, 1.0)
    clear_outside(mid, 2)
    stage(mid, wide, mid2, rows + 2, 2, 0.75, 0.25)
    clear_outside(mid2, 1)
    stage(mid2, wide, last, rows, 3, 1.0 / 3.0, 2.0 / 3.0)

    part = width // n_mem
    per_block = 128 // part
    lane = lax.broadcasted_iota(jnp.int32, (members, 128), 1) // part

    def choose(pieces, offset):
        out = pieces[0] if offset == 0 else pltpu.roll(pieces[0], (-offset * part) % 128, 1)
        for r in range(1, rows):
            turned = pltpu.roll(pieces[r], ((r - offset) * part) % 128, 1) if r != offset else pieces[r]
            out = jnp.where(lane == r, turned, out)
        return out

    def pack(j, _):
        columns = pl.ds(pl.multiple_of(j * 128, 128), 128)
        for f in range(fields):
            pieces = [last[r, f, :, columns] for r in range(rows)]
            for q in range(per_block):
                packed[j * per_block + q, :, pl.ds(f * 128, 128)] = choose(pieces, q)
        return 0

    lax.fori_loop(0, width // 128, pack, 0)

    def exchange(source, target, send_sem, recv_sem):
        def send(i, _):
            peer = lax.rem(me + 1 + lax.rem(i + n_mem // 2 - 1, n_mem - 1), n_mem)
            pltpu.make_async_remote_copy(
                src_ref=source.at[peer], dst_ref=target.at[me],
                send_sem=send_sem, recv_sem=recv_sem,
                device_id={"mem": peer}, device_id_type=MESH,
            ).start()
            return 0

        lax.fori_loop(0, n_mem - 1, send, 0)
        target[me] = source[me]
        others = pl.ds(0, n_mem - 1)
        pltpu.make_async_copy(target.at[others], target.at[others], recv_sem).wait()

    def drain(source, send_sem):
        others = pl.ds(0, n_mem - 1)
        pltpu.make_async_copy(source.at[others], source.at[others], send_sem).wait()

    exchange(packed, gathered, send_a, recv_a)

    total = n_mem * members
    cells = fields * rows * part
    values_all = gathered[...].reshape(total, cells)
    xbar = jnp.sum(values_all, axis=0, keepdims=True) * (1.0 / total)
    pert = values_all - xbar
    nobs = values_ref.shape[1]
    eye = (
        lax.broadcasted_iota(jnp.int32, (nobs, nobs), 0)
        == lax.broadcasted_iota(jnp.int32, (nobs, nobs), 1)
    )
    cell = cell_ref[...].astype(jnp.float32)
    cell_col = jnp.sum(jnp.where(eye, cell, 0.0), axis=1, keepdims=True).astype(jnp.int32)
    onehot = jnp.where(lax.broadcasted_iota(jnp.int32, (nobs, cells), 1) == cell_col, 1.0, 0.0)
    ypt = mm(onehot, pert, ((1,), (1,)))
    yp = mm(pert, onehot, ((1,), (1,)))
    kept, on_obs, common = analysis_weights(
        ypt, pert, onehot, xbar, values_ref[...], variance_ref[...],
        loop_ref[...].astype(jnp.float32), count_ref[...], float(total),
    )
    updated = kept * pert + mm(yp, on_obs) + common
    fresh[...] = updated.reshape(n_mem, members, cells)
    exchange(fresh, back, send_b, recv_b)

    def unpack(j, _):
        columns = pl.ds(pl.multiple_of(j * 128, 128), 128)
        for f in range(fields):
            pieces = [back[j * per_block + q, :, pl.ds(f * 128, 128)] for q in range(per_block)]
            for r in range(rows):
                o_ref[:, f, r, columns] = choose(pieces, r)
        return 0

    lax.fori_loop(0, width // 128, unpack, 0)
    drain(packed, send_a)
    drain(fresh, send_b)


def per_device(ensemble, obs_value, obs_var, obs_cell, obs_loop, obs_count):
    members, fields, rows, width = ensemble.shape
    n_mem = lax.axis_size("mem")
    cells = fields * rows * width // n_mem
    f32 = jnp.float32
    vmem = pl.BlockSpec(memory_space=pltpu.VMEM)
    return pl.pallas_call(
        kernel,
        out_shape=jax.ShapeDtypeStruct(ensemble.shape, f32),
        in_specs=[vmem] * 6,
        out_specs=vmem,
        scratch_shapes=[
            pltpu.VMEM((rows + 6, fields, members, width), f32),
            pltpu.VMEM((rows + 4, fields, members, width), f32),
            pltpu.VMEM((rows + 2, fields, members, width), f32),
            pltpu.VMEM((rows, fields, members, width), f32),
            pltpu.VMEM((n_mem, members, cells), f32),
            pltpu.VMEM((n_mem, members, cells), f32),
            pltpu.VMEM((n_mem, members, cells), f32),
            pltpu.VMEM((n_mem, members, cells), f32),
            pltpu.SemaphoreType.DMA((2,)),
            pltpu.SemaphoreType.DMA((2,)),
            pltpu.SemaphoreType.DMA,
            pltpu.SemaphoreType.DMA,
            pltpu.SemaphoreType.DMA,
            pltpu.SemaphoreType.DMA,
        ],
        compiler_params=pltpu.CompilerParams(collective_id=0, has_side_effects=True),
    )(
        ensemble, obs_value[0], obs_var[0], obs_cell[0], obs_loop[0], obs_count,
    )


def solution(mesh):
    placed = (
        P("mem", None, "lat", None),
        P(None, ("mem", "lat"), None),
        P(None, ("mem", "lat"), None),
        P(None, ("mem", "lat"), None),
        P(None, ("mem", "lat"), None),
        P(None, ("mem", "lat")),
    )
    return jax.shard_map(
        per_device,
        mesh=mesh,
        in_specs=placed,
        out_specs=P("mem", None, "lat", None),
        check_vma=False,
    )
```

time: 156 us -> 75.2 us (0.48)
  the two profiles are of different devices: /device:TPU:6 before, /device:TPU:1 now
where the time goes in v1:
time: 75.2 us; the launch traced here: 75 us
  Pallas kernels  72.5 us (96%)
  local copies, waits for them, and re-layouts  1.87 us (2%)
    pallas_call x1, Pallas kernels, per_device(): pl.pallas_call(kernel, out_shape=jax.ShapeDtypeStruct(ensemble.shape, f32...  72.5 us
    unnamed x1, local copies, waits for them, and re-layouts  1.87 us

profile of v1, /device:TPU:1, one launch (start us, length us, event | category | flops | bytes accessed | tf_op | source)
XLA Modules:
  0.0 75.0 jit_solution(2596510371870119376)
XLA Ops:
  0.7 72.5 %shard_map.64 = f32[8,4,4,1024]{3,2,1,0:T(4,128)} custom-call(f32[8,4,4,1024]{3,2,1,0:T(4,128)} %x_ref.1, f32[1,16]{1,0:T(1,128)} %bitcast.4, f32[1,16]{1,0:T(1,128)} %bitcast.5, s32[1,16]{1,0:T(1,128)} %bitcast.6, s32[1,16]{1,0:T(1,128)} %bitcast.7, s32[1,1]{1,0:T(1,128)S(6)} %copy.8.count_ref), custom_call_target="tpu_custom_call" | custom-call | tf_op jit(solution)/shard_map/pallas_call | solution.py:244
  73.1 1.9 %copy.9 = f32[8,4,4,1024]{3,2,1,0:T(4,128)} copy(f32[8,4,4,1024]{3,2,1,0:T(4,128)} %shard_map.64) | data formatting | bytes 1048576

commit v2 on v1

v2 whole, which is shorter than its diff:
```python
import jax
import jax.numpy as jnp
from jax import lax
from jax.experimental import pallas as pl
from jax.experimental.pallas import tpu as pltpu
from jax.sharding import PartitionSpec as P

MESH = pl.DeviceIdType.MESH
NSI = 5
DT = 0.15
VISC = 0.1
CHUNK = 2
HALO = 3


def mm(a, b, dims=((1,), (0,))):
    return lax.dot_general(
        a, b, (dims, ((), ())), precision=lax.Precision.HIGHEST, preferred_element_type=jnp.float32
    )


def analysis_weights(ypt, pert, onehot, xbar, values, variance, loop, count, members):
    nobs = ypt.shape[0]
    eye = (
        lax.broadcasted_iota(jnp.int32, (nobs, nobs), 0)
        == lax.broadcasted_iota(jnp.int32, (nobs, nobs), 1)
    )
    identity = jnp.where(eye, 1.0, 0.0)
    slots = lax.broadcasted_iota(jnp.int32, (1, nobs), 1)
    weight = jnp.where(slots < count, jnp.exp(-0.35 * loop) / variance, 0.0)

    def column(row):
        return jnp.sum(jnp.where(eye, row, 0.0), axis=1, keepdims=True)

    weight_col = column(weight)
    seen_mean = jnp.sum(onehot * xbar, axis=1, keepdims=True)
    innovation = column(values) - seen_mean
    cross = mm(ypt, pert)
    gram = mm(ypt, ypt, ((1,), (1,)))
    trace = jnp.sum(jnp.where(eye, gram * weight, 0.0), axis=(0, 1), keepdims=True)
    bound = members - 1.0 + 0.5 * trace
    a = (members - 1.0) / bound
    t = gram * weight / bound
    p0, p_m, p_h = a, a * identity + t, identity
    z0, z_m, z_h = jnp.ones_like(a), identity, jnp.zeros_like(identity)
    for repeat in range(NSI):
        g0 = 1.5 - 0.5 * p0
        g_m = 1.5 * identity - 0.5 * p_m
        g_h = -0.5 * p_h
        if repeat == 0:
            z_m, z_h, z0 = g_m, g_h, g0
            pg_m = mm(p_m, g_m)
            pg_h = g_m + p0 * g_h
        else:
            prod = mm(jnp.concatenate([p_m, p_h, z_m, z_h], axis=0), g_m)
            pg_m = prod[0:nobs]
            pg_h = prod[nobs : 2 * nobs] + p0 * g_h
            z_m = prod[2 * nobs : 3 * nobs]
            z_h = prod[3 * nobs :] + z0 * g_h
            z0 = z0 * g0
        if repeat < NSI - 1:
            prod = mm(jnp.concatenate([pg_m, pg_h], axis=0), g_m)
            p_m = prod[0:nobs]
            p_h = prod[nobs:] + (p0 * g0) * g_h
            p0 = p0 * g0 * g0
    spread = jnp.sqrt(a)
    step = mm(z_m, mm(z_m, innovation))
    shift_row = jnp.sum(weight_col * step * cross, axis=0, keepdims=True) / bound
    rows = mm((spread / bound) * weight_col * z_h, cross)
    return spread * z0, rows, xbar + shift_row


def kernel(
    x_ref, values_ref, variance_ref, cell_ref, loop_ref, count_ref, o_ref,
    wide, mid, mid2, packed, gathered, fresh, back,
    halo_send, halo_recv, send_a, recv_a, send_b, recv_b,
):
    n_mem, n_lat = lax.axis_size("mem"), lax.axis_size("lat")
    me, band = lax.axis_index("mem"), lax.axis_index("lat")
    members, fields, _, _ = x_ref.shape
    rows = 4
    chunks = members // CHUNK
    spans = packed.shape[2]
    held = fields // spans

    barrier = pltpu.get_barrier_semaphore()

    def greet(k, _):
        pl.semaphore_signal(
            barrier, inc=1, device_id={"mem": lax.rem(me + k, n_mem)}, device_id_type=MESH
        )
        return 0

    @pl.when(band < n_lat - 1)
    def _():
        pl.semaphore_signal(barrier, inc=1, device_id={"lat": band + 1}, device_id_type=MESH)

    @pl.when(band > 0)
    def _():
        pl.semaphore_signal(barrier, inc=1, device_id={"lat": band - 1}, device_id_type=MESH)

    lax.fori_loop(1, n_mem, greet, 0)

    def spread_rows(m, _):
        for f in range(fields):
            for r in range(rows):
                wide[m, HALO + r, f] = x_ref[m, f, pl.ds(r, 8, stride=rows), :]
        return 0

    lax.fori_loop(0, members, spread_rows, 0)

    beside = (band + n_lat - 1) // n_lat + (2 * n_lat - 2 - band) // n_lat
    pl.semaphore_wait(barrier, n_mem - 1 + beside)

    def upward(c):
        part = pl.ds(c * CHUNK, CHUNK)
        return pltpu.make_async_remote_copy(
            src_ref=wide.at[part, pl.ds(rows, HALO)], dst_ref=wide.at[part, pl.ds(0, HALO)],
            send_sem=halo_send.at[0, c], recv_sem=halo_recv.at[0, c],
            device_id={"lat": band + 1}, device_id_type=MESH,
        )

    def downward(c):
        part = pl.ds(c * CHUNK, CHUNK)
        return pltpu.make_async_remote_copy(
            src_ref=wide.at[part, pl.ds(HALO, HALO)], dst_ref=wide.at[part, pl.ds(HALO + rows, HALO)],
            send_sem=halo_send.at[1, c], recv_sem=halo_recv.at[1, c],
            device_id={"lat": band - 1}, device_id_type=MESH,
        )

    @pl.when(band < n_lat - 1)
    def _():
        for c in range(chunks):
            upward(c).start()

    @pl.when(band > 0)
    def _():
        for c in range(chunks):
            downward(c).start()

    lane = lax.broadcasted_iota(jnp.int32, (8, 128), 1)
    last_lane, first_lane = lane == 127, lane == 0
    quarter = lane // 32
    has_south, has_north = band > 0, band < n_lat - 1

    def east(c):
        turned = pltpu.roll(c, 127, 1)
        return jnp.where(last_lane, pltpu.roll(turned, 7, 0), turned)

    def west(c):
        turned = pltpu.roll(c, 1, 1)
        return jnp.where(first_lane, pltpu.roll(turned, 1, 0), turned)

    def stage(source, base, count, weight_base, weight_mid):
        scale = weight_mid * DT
        for i in range(count):
            u = 0.5 * scale * source(i + 1, 0)
            v = 0.5 * scale * source(i + 1, 1)
            drag = scale * VISC
            east_w, west_w, north_w, south_w = drag - u, drag + u, drag - v, drag + v
            for f in range(fields):
                c = source(i + 1, f)
                total = (weight_mid - 4.0 * drag) * c
                total += north_w * source(i + 2, f) + south_w * source(i, f)
                total += east_w * east(c) + west_w * west(c)
                if weight_base:
                    total += weight_base * base(i, f)
                yield i, f, total

    def inside(value, i, extra):
        if i < extra:
            return jnp.where(has_south, value, 0.0)
        if i >= extra + rows:
            return jnp.where(has_north, value, 0.0)
        return value

    def choose(pieces, offset):
        out = None
        for r in range(rows):
            turned = pltpu.roll(pieces[r], ((r - offset) * 32) % 128, 1) if r != offset else pieces[r]
            out = turned if out is None else jnp.where(quarter == r, turned, out)
        return out

    def position(slot):
        return lax.rem(slot, rows), pl.ds(pl.multiple_of((slot // rows) * 8, 8), 8)

    def advance_member(c, ml):
        m = c * CHUNK + ml

        def from_wide(i, f):
            return inside(wide[m, i, f], i, HALO)

        for i, f, value in stage(from_wide, None, rows + 4, 0.0, 1.0):
            mid[i, f] = inside(value, i, 2)
        for i, f, value in stage(lambda i, f: mid[i, f], lambda i, f: from_wide(i + 2, f), rows + 2, 0.75, 0.25):
            mid2[i, f] = inside(value, i, 1)
        result = {}
        for i, f, value in stage(lambda i, f: mid2[i, f], lambda i, f: wide[m, i + 3, f], rows, 1.0 / 3.0, 2.0 / 3.0):
            result[i, f] = value
        for f in range(fields):
            pieces = [result[r, f] for r in range(rows)]
            for q in range(rows):
                packed[c, q, f // held, pl.ds(ml * held + f % held, 8, stride=8), :] = choose(pieces, q)

    mine, others = pl.ds(pl.multiple_of(me * 8, 8), 8), pl.ds(0, (n_mem - 1) * 8)
    my_q, my_rows = position(me)

    def peer_of(i):
        return lax.rem(me + 1 + lax.rem(i + n_mem // 2 - 1, n_mem - 1), n_mem)

    def chunk_step(c, _):
        @pl.when(has_south)
        def _():
            upward(c).wait_recv()

        @pl.when(has_north)
        def _():
            downward(c).wait_recv()

        for ml in range(CHUNK):
            advance_member(c, ml)

        def send(i, _):
            peer = peer_of(i)
            q, place = position(peer)
            pltpu.make_async_remote_copy(
                src_ref=packed.at[c, q, :, place], dst_ref=gathered.at[c, :, mine],
                send_sem=send_a.at[c], recv_sem=recv_a.at[c],
                device_id={"mem": peer}, device_id_type=MESH,
            ).start()
            return 0

        lax.fori_loop(0, n_mem - 1, send, 0)
        gathered[c, :, mine] = packed[c, my_q, :, my_rows]
        return 0

    lax.fori_loop(0, chunks, chunk_step, 0)

    for c in range(chunks):
        pltpu.make_async_copy(gathered.at[c, :, others], gathered.at[c, :, others], recv_a.at[c]).wait()

    total = n_mem * members
    values_all = jnp.concatenate(
        [
            jnp.concatenate(
                [gathered[c, f // held, pl.ds(f % held, n_mem * CHUNK, stride=held), :] for f in range(fields)],
                axis=1,
            )
            for c in range(chunks)
        ],
        axis=0,
    )
    cells = values_all.shape[1]
    xbar = jnp.sum(values_all, axis=0, keepdims=True) * (1.0 / total)
    pert = values_all - xbar
    nobs = values_ref.shape[1]
    eye = (
        lax.broadcasted_iota(jnp.int32, (nobs, nobs), 0)
        == lax.broadcasted_iota(jnp.int32, (nobs, nobs), 1)
    )
    cell = cell_ref[...].astype(jnp.float32)
    cell_col = jnp.sum(jnp.where(eye, cell, 0.0), axis=1, keepdims=True).astype(jnp.int32)
    onehot = jnp.where(lax.broadcasted_iota(jnp.int32, (nobs, cells), 1) == cell_col, 1.0, 0.0)
    ypt = mm(onehot, pert, ((1,), (1,)))
    yp = mm(pert, onehot, ((1,), (1,)))
    kept, on_obs, common = analysis_weights(
        ypt, pert, onehot, xbar, values_ref[...], variance_ref[...],
        loop_ref[...].astype(jnp.float32), count_ref[...], float(total),
    )
    updated = kept * pert + mm(yp, on_obs) + common
    size = n_mem * CHUNK
    for c in range(chunks):
        for f in range(fields):
            fresh[c, f // held, pl.ds(f % held, size, stride=held), :] = updated[
                c * size : (c + 1) * size, f * 128 : (f + 1) * 128
            ]

    def send_back(i, _):
        peer = peer_of(i)
        place = pl.ds(pl.multiple_of(peer * 8, 8), 8)
        pltpu.make_async_remote_copy(
            src_ref=fresh.at[:, :, place], dst_ref=back.at[:, my_q, :, my_rows],
            send_sem=send_b, recv_sem=recv_b,
            device_id={"mem": peer}, device_id_type=MESH,
        ).start()
        return 0

    lax.fori_loop(0, n_mem - 1, send_back, 0)
    back[:, my_q, :, my_rows] = fresh[:, :, mine]

    for c in range(chunks):
        pltpu.make_async_copy(gathered.at[c, :, others], gathered.at[c, :, others], send_a.at[c]).wait()

    @pl.when(has_north)
    def _():
        for c in range(chunks):
            upward(c).wait_send()

    @pl.when(has_south)
    def _():
        for c in range(chunks):
            downward(c).wait_send()

    everyone = fresh.at[:, :, others]
    pltpu.make_async_copy(everyone, everyone, recv_b).wait()

    for m in range(members):
        c, ml = m // CHUNK, m % CHUNK
        for f in range(fields):
            pieces = [back[c, q, f // held, pl.ds(ml * held + f % held, 8, stride=8), :] for q in range(rows)]
            for r in range(rows):
                o_ref[m, f, pl.ds(r, 8, stride=rows), :] = choose(pieces, r)

    pltpu.make_async_copy(everyone, everyone, send_b).wait()


def per_device(ensemble, obs_value, obs_var, obs_cell, obs_loop, obs_count):
    members, fields, rows, width = ensemble.shape
    n_mem = lax.axis_size("mem")
    f32 = jnp.float32
    vmem = pl.BlockSpec(memory_space=pltpu.VMEM)
    blocks = width // 128
    chunks = members // CHUNK
    spans = fields * CHUNK // 8
    view = (
        ensemble.reshape(members, fields, rows, blocks, 128)
        .transpose(0, 1, 3, 2, 4)
        .reshape(members, fields, blocks * rows, 128)
    )
    out = pl.pallas_call(
        kernel,
        out_shape=jax.ShapeDtypeStruct(view.shape, f32),
        in_specs=[vmem] * 6,
        out_specs=vmem,
        scratch_shapes=[
            pltpu.VMEM((members, rows + 2 * HALO, fields, 8, 128), f32),
            pltpu.VMEM((rows + 4, fields, 8, 128), f32),
            pltpu.VMEM((rows + 2, fields, 8, 128), f32),
            pltpu.VMEM((chunks, rows, spans, 64, 128), f32),
            pltpu.VMEM((chunks, spans, n_mem * 8, 128), f32),
            pltpu.VMEM((chunks, spans, n_mem * 8, 128), f32),
            pltpu.VMEM((chunks, rows, spans, 64, 128), f32),
            pltpu.SemaphoreType.DMA((2, chunks)),
            pltpu.SemaphoreType.DMA((2, chunks)),
            pltpu.SemaphoreType.DMA((chunks,)),
            pltpu.SemaphoreType.DMA((chunks,)),
            pltpu.SemaphoreType.DMA,
            pltpu.SemaphoreType.DMA,
        ],
        compiler_params=pltpu.CompilerParams(collective_id=0, has_side_effects=True),
    )(
        view, obs_value[0], obs_var[0], obs_cell[0], obs_loop[0], obs_count,
    )
    return (
        out.reshape(members, fields, blocks, rows, 128)
        .transpose(0, 1, 3, 2, 4)
        .reshape(ensemble.shape)
    )


def solution(mesh):
    placed = (
        P("mem", None, "lat", None),
        P(None, ("mem", "lat"), None),
        P(None, ("mem", "lat"), None),
        P(None, ("mem", "lat"), None),
        P(None, ("mem", "lat"), None),
        P(None, ("mem", "lat")),
    )
    return jax.shard_map(
        per_device,
        mesh=mesh,
        in_specs=placed,
        out_specs=P("mem", None, "lat", None),
        check_vma=False,
    )
```

time: 75.2 us -> 67.5 us (0.90)
  the two profiles are of different devices: /device:TPU:1 before, /device:TPU:11 now
where the time goes in v2:
time: 67.5 us; the launch traced here: 67.3 us
  Pallas kernels  64.7 us (96%)
  local copies, waits for them, and re-layouts  1.87 us (3%)
    pallas_call x1, Pallas kernels, per_device(): pl.pallas_call(kernel, out_shape=jax.ShapeDtypeStruct(view.shape, f32), i...  64.7 us
    unnamed x1, local copies, waits for them, and re-layouts  1.87 us

profile of v2, /device:TPU:11, one launch (start us, length us, event | category | flops | bytes accessed | tf_op | source)
XLA Modules:
  0.0 67.3 jit_solution(4757830477291924314)
XLA Ops:
  0.7 64.7 %shard_map.64 = f32[8,4,32,128]{3,2,1,0:T(8,128)} custom-call(f32[8,4,32,128]{3,2,1,0:T(8,128)} %bitcast.15, f32[1,16]{1,0:T(1,128)} %bitcast.16, f32[1,16]{1,0:T(1,128)} %bitcast.17, s32[1,16]{1,0:T(1,128)} %bitcast.18, s32[1,16]{1,0:T(1,128)} %bitcast.19, s32[1,1]{1,0:T(1,128)S(6)} %copy.10.count_ref), custom_call_target="tpu_custom_call" | custom-call | tf_op jit(solution)/shard_map/pallas_call | solution.py:330
  65.4 1.9 %copy.11 = f32[8,4,4,1024]{3,2,1,0:T(4,128)} copy(f32[8,4,4,1024]{3,2,1,0:T(4,128)} %bitcast.14) | data formatting | bytes 1048576

commit v3 on v2

--- a/solution.py
+++ b/solution.py
@@ -13,67 +13,81 @@
 HALO = 3
 
 
+def choose(pieces, offset, quarter):
+    out = None
+    for r, piece in enumerate(pieces):
+        turned = pltpu.roll(piece, ((r - offset) * 32) % 128, 1) if r != offset else piece
+        out = turned if out is None else jnp.where(quarter == r, turned, out)
+    return out
+
+
+def split(x):
+    high = x.astype(jnp.bfloat16)
+    return high, (x - high.astype(jnp.float32)).astype(jnp.bfloat16)
+
+
+def dot(a, b, dims=((1,), (0,))):
+    return lax.dot_general(a, b, (dims, ((), ())), preferred_element_type=jnp.float32)
+
+
 def mm(a, b, dims=((1,), (0,))):
-    return lax.dot_general(
-        a, b, (dims, ((), ())), precision=lax.Precision.HIGHEST, preferred_element_type=jnp.float32
-    )
-
-
-def analysis_weights(ypt, pert, onehot, xbar, values, variance, loop, count, members):
-    nobs = ypt.shape[0]
-    eye = (
-        lax.broadcasted_iota(jnp.int32, (nobs, nobs), 0)
-        == lax.broadcasted_iota(jnp.int32, (nobs, nobs), 1)
-    )
+    return dot(a[0], b[0], dims) + (dot(a[0], b[1], dims) + dot(a[1], b[0], dims))
+
+
+def product(a, b):
+    terms = [a[:, k : k + 1] * b[k : k + 1, :] for k in range(a.shape[1])]
+    while len(terms) > 1:
+        terms = [x + y for x, y in zip(terms[::2], terms[1::2])]
+    return terms[0]
+
+
+def diagonal_of(size):
+    return lax.broadcasted_iota(jnp.int32, (size, size), 0) == lax.broadcasted_iota(
+        jnp.int32, (size, size), 1
+    )
+
+
+def as_column(row, eye):
+    return jnp.sum(jnp.where(eye, row, 0.0), axis=1, keepdims=True)
+
+
+def as_row(column, eye):
+    return jnp.sum(jnp.where(eye, column, 0.0), axis=0, keepdims=True)
+
+
+def solve(gram, innovation, weight, eye, members):
+    nobs = gram.shape[0]
+    weight_col = as_column(weight, eye)
+    trace = jnp.sum(jnp.where(eye, gram * weight, 0.0), axis=(0, 1), keepdims=True)
+    inverse = 1.0 / (members - 1.0 + 0.5 * trace)
+    a = (members - 1.0) * inverse
+    t = gram * (weight * inverse)
     identity = jnp.where(eye, 1.0, 0.0)
-    slots = lax.broadcasted_iota(jnp.int32, (1, nobs), 1)
-    weight = jnp.where(slots < count, jnp.exp(-0.35 * loop) / variance, 0.0)
-
-    def column(row):
-        return jnp.sum(jnp.where(eye, row, 0.0), axis=1, keepdims=True)
-
-    weight_col = column(weight)
-    seen_mean = jnp.sum(onehot * xbar, axis=1, keepdims=True)
-    innovation = column(values) - seen_mean
-    cross = mm(ypt, pert)
-    gram = mm(ypt, ypt, ((1,), (1,)))
-    trace = jnp.sum(jnp.where(eye, gram * weight, 0.0), axis=(0, 1), keepdims=True)
-    bound = members - 1.0 + 0.5 * trace
-    a = (members - 1.0) / bound
-    t = gram * weight / bound
-    p0, p_m, p_h = a, a * identity + t, identity
-    z0, z_m, z_h = jnp.ones_like(a), identity, jnp.zeros_like(identity)
+    group = lax.broadcasted_iota(jnp.int32, (nobs, 4 * nobs), 1) // nobs
+    state = jnp.concatenate([a * identity + t, identity, identity, jnp.zeros_like(t)], axis=1)
+    p0, z0 = a, jnp.ones_like(a)
     for repeat in range(NSI):
         g0 = 1.5 - 0.5 * p0
-        g_m = 1.5 * identity - 0.5 * p_m
-        g_h = -0.5 * p_h
-        if repeat == 0:
-            z_m, z_h, z0 = g_m, g_h, g0
-            pg_m = mm(p_m, g_m)
-            pg_h = g_m + p0 * g_h
-        else:
-            prod = mm(jnp.concatenate([p_m, p_h, z_m, z_h], axis=0), g_m)
-            pg_m = prod[0:nobs]
-            pg_h = prod[nobs : 2 * nobs] + p0 * g_h
-            z_m = prod[2 * nobs : 3 * nobs]
-            z_h = prod[3 * nobs :] + z0 * g_h
-            z0 = z0 * g0
+        g = 1.5 * identity - 0.5 * state[:, :nobs]
+        h = state[:, nobs : 2 * nobs]
+        spread_h = jnp.concatenate([h, h, h, h], axis=1)
+        along = jnp.where(group == 1, -0.5 * p0, jnp.where(group == 3, -0.5 * z0, 0.0))
+        state = product(g, state) + along * spread_h
+        z0 = z0 * g0
         if repeat < NSI - 1:
-            prod = mm(jnp.concatenate([pg_m, pg_h], axis=0), g_m)
-            p_m = prod[0:nobs]
-            p_h = prod[nobs:] + (p0 * g0) * g_h
+            again = product(g, state) + jnp.where(group == 1, -0.5 * p0 * g0, 0.0) * spread_h
+            state = jnp.where(group < 2, again, state)
             p0 = p0 * g0 * g0
-    spread = jnp.sqrt(a)
-    step = mm(z_m, mm(z_m, innovation))
-    shift_row = jnp.sum(weight_col * step * cross, axis=0, keepdims=True) / bound
-    rows = mm((spread / bound) * weight_col * z_h, cross)
-    return spread * z0, rows, xbar + shift_row
+    z = state[:, 2 * nobs : 3 * nobs]
+    root = jnp.sqrt(a)
+    shift = weight_col * product(z, product(z, innovation)) * inverse
+    return root * z0, (root * inverse) * weight_col * state[:, 3 * nobs :], shift
 
 
 def kernel(
     x_ref, values_ref, variance_ref, cell_ref, loop_ref, count_ref, o_ref,
-    wide, mid, mid2, packed, gathered, fresh, back,
-    halo_send, halo_recv, send_a, recv_a, send_b, recv_b,
+    wide, mid, mid2, packed, gathered, fresh, centred,
+    halo_send, halo_recv, send_a, recv_a, send_b, recv_b, own_b,
 ):
     n_mem, n_lat = lax.axis_size("mem"), lax.axis_size("lat")
     me, band = lax.axis_index("mem"), lax.axis_index("lat")
@@ -174,13 +188,6 @@
             return jnp.where(has_north, value, 0.0)
         return value
 
-    def choose(pieces, offset):
-        out = None
-        for r in range(rows):
-            turned = pltpu.roll(pieces[r], ((r - offset) * 32) % 128, 1) if r != offset else pieces[r]
-            out = turned if out is None else jnp.where(quarter == r, turned, out)
-        return out
-
     def position(slot):
         return lax.rem(slot, rows), pl.ds(pl.multiple_of((slot // rows) * 8, 8), 8)
 
@@ -200,13 +207,19 @@
         for f in range(fields):
             pieces = [result[r, f] for r in range(rows)]
             for q in range(rows):
-                packed[c, q, f // held, pl.ds(ml * held + f % held, 8, stride=8), :] = choose(pieces, q)
+                packed[c, q, f // held, pl.ds(ml * held + f % held, 8, stride=8), :] = choose(pieces, q, quarter)
 
     mine, others = pl.ds(pl.multiple_of(me * 8, 8), 8), pl.ds(0, (n_mem - 1) * 8)
     my_q, my_rows = position(me)
 
     def peer_of(i):
-        return lax.rem(me + 1 + lax.rem(i + n_mem // 2 - 1, n_mem - 1), n_mem)
+        step, kind = i // 4, lax.rem(i, 4)
+        odd = lax.rem(step, 2)
+        dy = n_mem // 8 + (step // 2) * (1 - odd) - ((step + 1) // 2) * odd
+        y = lax.rem(me // 4 + dy, n_mem // 4)
+        x = lax.rem(lax.rem(me, 4) // 2 + 1 - kind // 2, 2)
+        core = lax.rem(lax.rem(me, 2) + 1 - lax.rem(kind, 2), 2)
+        return y * 4 + x * 2 + core
 
     def chunk_step(c, _):
         @pl.when(has_south)
@@ -236,57 +249,73 @@
 
     lax.fori_loop(0, chunks, chunk_step, 0)
 
+    nobs = values_ref.shape[1]
+    eye = diagonal_of(nobs)
+    cells = fields * 128
+    cell_col = as_column(cell_ref[...].astype(jnp.float32), eye).astype(jnp.int32)
+    is_cell = lax.broadcasted_iota(jnp.int32, (nobs, cells), 1) == cell_col
+    onehot = jnp.where(is_cell, 1.0, 0.0)
+    pick = onehot.astype(jnp.bfloat16)
+    slots = lax.broadcasted_iota(jnp.int32, (1, nobs), 1)
+    decay = jnp.exp(-0.35 * loop_ref[...].astype(jnp.float32)) / variance_ref[...]
+    weight = jnp.where(slots < count_ref[...], decay, 0.0)
+
+    total = n_mem * members
+    size = n_mem * CHUNK
+    seen_parts = []
     for c in range(chunks):
         pltpu.make_async_copy(gathered.at[c, :, others], gathered.at[c, :, others], recv_a.at[c]).wait()
-
-    total = n_mem * members
-    values_all = jnp.concatenate(
-        [
-            jnp.concatenate(
-                [gathered[c, f // held, pl.ds(f % held, n_mem * CHUNK, stride=held), :] for f in range(fields)],
-                axis=1,
-            )
-            for c in range(chunks)
-        ],
-        axis=0,
-    )
-    cells = values_all.shape[1]
-    xbar = jnp.sum(values_all, axis=0, keepdims=True) * (1.0 / total)
-    pert = values_all - xbar
-    nobs = values_ref.shape[1]
-    eye = (
-        lax.broadcasted_iota(jnp.int32, (nobs, nobs), 0)
-        == lax.broadcasted_iota(jnp.int32, (nobs, nobs), 1)
-    )
-    cell = cell_ref[...].astype(jnp.float32)
-    cell_col = jnp.sum(jnp.where(eye, cell, 0.0), axis=1, keepdims=True).astype(jnp.int32)
-    onehot = jnp.where(lax.broadcasted_iota(jnp.int32, (nobs, cells), 1) == cell_col, 1.0, 0.0)
-    ypt = mm(onehot, pert, ((1,), (1,)))
-    yp = mm(pert, onehot, ((1,), (1,)))
-    kept, on_obs, common = analysis_weights(
-        ypt, pert, onehot, xbar, values_ref[...], variance_ref[...],
-        loop_ref[...].astype(jnp.float32), count_ref[...], float(total),
-    )
-    updated = kept * pert + mm(yp, on_obs) + common
-    size = n_mem * CHUNK
+        block = jnp.concatenate(
+            [gathered[c, f // held, pl.ds(f % held, size, stride=held), :] for f in range(fields)], axis=1
+        )
+        if c == 0:
+            origin = jnp.sum(block, axis=0, keepdims=True) * (1.0 / size)
+        moved = block - origin
+        centred[c] = moved
+        parts = split(moved)
+        seen = dot(parts[0], pick, ((1,), (1,))) + dot(parts[1], pick, ((1,), (1,)))
+        seen_t = dot(pick, parts[0], ((1,), (1,))) + dot(pick, parts[1], ((1,), (1,)))
+        turned = split(seen_t)
+        seen_parts.append(split(seen))
+        cross_c = mm(turned, parts)
+        gram_c = mm(turned, turned, ((1,), (1,)))
+        sum_c = jnp.sum(moved, axis=0, keepdims=True)
+        if c == 0:
+            cross, gram, summed = cross_c, gram_c, sum_c
+        else:
+            cross, gram, summed = cross + cross_c, gram + gram_c, summed + sum_c
+
+    offset = summed * (1.0 / total)
+    offset_seen = jnp.sum(onehot * offset, axis=1, keepdims=True)
+    origin_seen = jnp.sum(onehot * origin, axis=1, keepdims=True)
+    cross = cross - (float(total) * offset_seen) * offset
+    gram = gram - (float(total) * offset_seen) * as_row(offset_seen, eye)
+    innovation = as_column(values_ref[...], eye) - (origin_seen + offset_seen)
+    kept, on_cross, shift = solve(gram, innovation, weight, eye, float(total))
+    rows_seen = product(on_cross, cross)
+    common = (
+        origin + (1.0 - kept) * offset
+        + jnp.sum(shift * cross - offset_seen * rows_seen, axis=0, keepdims=True)
+    )
+    rows_parts = split(rows_seen)
     for c in range(chunks):
+        updated = kept * centred[c] + (mm(seen_parts[c], rows_parts) + common)
         for f in range(fields):
-            fresh[c, f // held, pl.ds(f % held, size, stride=held), :] = updated[
-                c * size : (c + 1) * size, f * 128 : (f + 1) * 128
-            ]
-
-    def send_back(i, _):
-        peer = peer_of(i)
-        place = pl.ds(pl.multiple_of(peer * 8, 8), 8)
-        pltpu.make_async_remote_copy(
-            src_ref=fresh.at[:, :, place], dst_ref=back.at[:, my_q, :, my_rows],
-            send_sem=send_b, recv_sem=recv_b,
-            device_id={"mem": peer}, device_id_type=MESH,
-        ).start()
-        return 0
-
-    lax.fori_loop(0, n_mem - 1, send_back, 0)
-    back[:, my_q, :, my_rows] = fresh[:, :, mine]
+            fresh[c, f // held, pl.ds(f % held, size, stride=held), :] = updated[:, f * 128 : (f + 1) * 128]
+
+        def send_back(i, _):
+            peer = peer_of(i)
+            place = pl.ds(pl.multiple_of(peer * 8, 8), 8)
+            pltpu.make_async_remote_copy(
+                src_ref=fresh.at[c, :, place], dst_ref=o_ref.at[c, my_q, :, my_rows],
+                send_sem=send_b.at[c], recv_sem=recv_b.at[c],
+                device_id={"mem": peer}, device_id_type=MESH,
+            ).start()
+            return 0
+
+        lax.fori_loop(0, n_mem - 1, send_back, 0)
+    own = pltpu.make_async_copy(fresh.at[:, :, mine], o_ref.at[:, my_q, :, my_rows], own_b)
+    own.start()
 
     for c in range(chunks):
         pltpu.make_async_copy(gathered.at[c, :, others], gathered.at[c, :, others], send_a.at[c]).wait()
@@ -301,17 +330,22 @@
         for c in range(chunks):
             downward(c).wait_send()
 
-    everyone = fresh.at[:, :, others]
-    pltpu.make_async_copy(everyone, everyone, recv_b).wait()
-
-    for m in range(members):
-        c, ml = m // CHUNK, m % CHUNK
+    own.wait()
+    for c in range(chunks):
+        pltpu.make_async_copy(fresh.at[c, :, others], fresh.at[c, :, others], send_b.at[c]).wait()
+        pltpu.make_async_copy(fresh.at[c, :, others], fresh.at[c, :, others], recv_b.at[c]).wait()
+
+
+def unpack_kernel(back_ref, o_ref):
+    rows, spans = back_ref.shape[1], back_ref.shape[2]
+    fields = o_ref.shape[1]
+    held = fields // spans
+    quarter = lax.broadcasted_iota(jnp.int32, (8, 128), 1) // 32
+    for ml in range(CHUNK):
         for f in range(fields):
-            pieces = [back[c, q, f // held, pl.ds(ml * held + f % held, 8, stride=8), :] for q in range(rows)]
+            pieces = [back_ref[0, q, f // held, pl.ds(ml * held + f % held, 8, stride=8), :] for q in range(rows)]
             for r in range(rows):
-                o_ref[m, f, pl.ds(r, 8, stride=rows), :] = choose(pieces, r)
-
-    pltpu.make_async_copy(everyone, everyone, send_b).wait()
+                o_ref[ml, f, pl.ds(r, 8, stride=rows), :] = choose(pieces, r, quarter)
 
 
 def per_device(ensemble, obs_value, obs_var, obs_cell, obs_loop, obs_count):
@@ -327,11 +361,11 @@
         .transpose(0, 1, 3, 2, 4)
         .reshape(members, fields, blocks * rows, 128)
     )
-    out = pl.pallas_call(
+    back = pl.pallas_call(
         kernel,
-        out_shape=jax.ShapeDtypeStruct(view.shape, f32),
+        out_shape=jax.ShapeDtypeStruct((chunks, rows, spans, 64, 128), f32),
         in_specs=[vmem] * 6,
-        out_specs=vmem,
+        out_specs=pl.BlockSpec(memory_space=pl.ANY),
         scratch_shapes=[
             pltpu.VMEM((members, rows + 2 * HALO, fields, 8, 128), f32),
             pltpu.VMEM((rows + 4, fields, 8, 128), f32),
@@ -339,18 +373,26 @@
             pltpu.VMEM((chunks, rows, spans, 64, 128), f32),
             pltpu.VMEM((chunks, spans, n_mem * 8, 128), f32),
             pltpu.VMEM((chunks, spans, n_mem * 8, 128), f32),
-            pltpu.VMEM((chunks, rows, spans, 64, 128), f32),
+            pltpu.VMEM((chunks, n_mem * CHUNK, fields * 128), f32),
             pltpu.SemaphoreType.DMA((2, chunks)),
             pltpu.SemaphoreType.DMA((2, chunks)),
             pltpu.SemaphoreType.DMA((chunks,)),
             pltpu.SemaphoreType.DMA((chunks,)),
-            pltpu.SemaphoreType.DMA,
+            pltpu.SemaphoreType.DMA((chunks,)),
+            pltpu.SemaphoreType.DMA((chunks,)),
             pltpu.SemaphoreType.DMA,
         ],
         compiler_params=pltpu.CompilerParams(collective_id=0, has_side_effects=True),
     )(
         view, obs_value[0], obs_var[0], obs_cell[0], obs_loop[0], obs_count,
     )
+    out = pl.pallas_call(
+        unpack_kernel,
+        grid=(chunks,),
+        out_shape=jax.ShapeDtypeStruct(view.shape, f32),
+        in_specs=[pl.BlockSpec((1, rows, spans, 64, 128), lambda c: (c, 0, 0, 0, 0))],
+        out_specs=pl.BlockSpec((CHUNK, fields, blocks * rows, 128), lambda c: (c, 0, 0, 0)),
+    )(back)
     return (
         out.reshape(members, fields, blocks, rows, 128)
         .transpose(0, 1, 3, 2, 4)

time: 67.5 us -> 64.9 us (0.961)
  the two profiles are of different devices: /device:TPU:11 before, /device:TPU:3 now
where the time goes in v3:
time: 64.9 us; the launch traced here: 64.7 us
  Pallas kernels  64 us (99%)
  between operations  0.66 us (1%)
    pallas_call x1, Pallas kernels, per_device(): pl.pallas_call(kernel, out_shape=jax.ShapeDtypeStruct((chunks, rows, span...  60.6 us
    pallas_call x1, Pallas kernels, per_device(): pl.pallas_call(unpack_kernel, grid=(chunks,), out_shape=jax.ShapeDtypeStr...  3.48 us

profile of v3, /device:TPU:3, one launch (start us, length us, event | category | flops | bytes accessed | tf_op | source)
XLA Modules:
  0.0 64.7 jit_solution(2453070610693110289)
XLA Ops:
  0.7 60.6 %shard_map.64.back_ref = f32[4,4,1,64,128]{4,3,2,1,0:T(8,128)} custom-call(f32[8,4,32,128]{3,2,1,0:T(8,128)} %bitcast.14, f32[1,16]{1,0:T(1,128)} %bitcast.15, f32[1,16]{1,0:T(1,128)} %bitcast.16, s32[1,16]{1,0:T(1,128)} %bitcast.17, s32[1,16]{1,0:T(1,128)} %bitcast.18, s32[1,1]{1,0:T(1,128)S(6)} %copy.9.count_ref), custom_call_target="tpu_custom_call" | custom-call | tf_op jit(solution)/shard_map/pallas_call | solution.py:364
  61.2 3.5 %shard_map.65 = f32[8,4,32,128]{3,2,1,0:T(8,128)} custom-call(f32[4,4,1,64,128]{4,3,2,1,0:T(8,128)} %shard_map.64.back_ref), custom_call_target="tpu_custom_call" | custom-call | tf_op jit(solution)/shard_map/pallas_call | solution.py:389

commit v4 on v3

--- a/solution.py
+++ b/solution.py
@@ -85,25 +85,54 @@
 
 
 def kernel(
-    x_ref, values_ref, variance_ref, cell_ref, loop_ref, count_ref, o_ref,
-    wide, mid, mid2, packed, gathered, fresh, centred,
-    halo_send, halo_recv, send_a, recv_a, send_b, recv_b, own_b,
+    x_hbm, values_hbm, variance_hbm, cell_hbm, loop_hbm, count_hbm, o_ref,
+    x_ref, values_ref, variance_ref, cell_ref, loop_ref, count_ref, wide, mid, mid2, packed, gathered, fresh, centred,
+    halo_send, halo_recv, send_a, recv_a, send_b, recv_b, own_b, load_x, load_small,
 ):
     n_mem, n_lat = lax.axis_size("mem"), lax.axis_size("lat")
     me, band = lax.axis_index("mem"), lax.axis_index("lat")
-    members, fields, _, _ = x_ref.shape
+    members, fields, _, _ = x_hbm.shape
     rows = 4
     chunks = members // CHUNK
     spans = packed.shape[2]
     held = fields // spans
 
+    loads = [
+        pltpu.make_async_copy(
+            x_hbm.at[pl.ds(c * CHUNK, CHUNK)], x_ref.at[pl.ds(c * CHUNK, CHUNK)], load_x.at[c]
+        )
+        for c in range(chunks)
+    ]
+    small = [
+        pltpu.make_async_copy(source, target, load_small.at[k])
+        for k, (source, target) in enumerate(
+            (
+                (values_hbm, values_ref), (variance_hbm, variance_ref), (cell_hbm, cell_ref),
+                (loop_hbm, loop_ref), (count_hbm, count_ref),
+            )
+        )
+    ]
+    for load in loads + small:
+        load.start()
+
+    ring = n_mem // 4
+    my_y = me // 4
+    my_x = (me - 4 * my_y) // 2
+    my_core = me - 4 * my_y - 2 * my_x
+    ys = [my_y] + [jnp.where(my_y + k >= ring, my_y + k - ring, my_y + k) for k in range(1, ring)]
+    xs = (my_x, 1 - my_x)
+    cores = (my_core, 1 - my_core)
+    order = [ring // 2]
+    for k in range(1, ring // 2):
+        order += [ring // 2 - k, ring // 2 + k]
+    peers = [
+        (ys[k], 2 * xs[x] + cores[core])
+        for k in order + [0]
+        for x, core in ((1, 1), (1, 0), (0, 1), (0, 0))
+        if k or x or core
+    ]
+
     barrier = pltpu.get_barrier_semaphore()
-
-    def greet(k, _):
-        pl.semaphore_signal(
-            barrier, inc=1, device_id={"mem": lax.rem(me + k, n_mem)}, device_id_type=MESH
-        )
-        return 0
 
     @pl.when(band < n_lat - 1)
     def _():
@@ -113,16 +142,17 @@
     def _():
         pl.semaphore_signal(barrier, inc=1, device_id={"lat": band - 1}, device_id_type=MESH)
 
-    lax.fori_loop(1, n_mem, greet, 0)
-
-    def spread_rows(m, _):
-        for f in range(fields):
-            for r in range(rows):
-                wide[m, HALO + r, f] = x_ref[m, f, pl.ds(r, 8, stride=rows), :]
-        return 0
-
-    lax.fori_loop(0, members, spread_rows, 0)
-
+    for y, q in peers:
+        pl.semaphore_signal(barrier, inc=1, device_id={"mem": 4 * y + q}, device_id_type=MESH)
+
+    def spread_rows(c):
+        loads[c].wait()
+        for m in range(c * CHUNK, (c + 1) * CHUNK):
+            for f in range(fields):
+                for r in range(rows):
+                    wide[m, HALO + r, f] = x_ref[m, f, pl.ds(r, 8, stride=rows), :]
+
+    spread_rows(0)
     beside = (band + n_lat - 1) // n_lat + (2 * n_lat - 2 - band) // n_lat
     pl.semaphore_wait(barrier, n_mem - 1 + beside)
 
@@ -142,14 +172,16 @@
             device_id={"lat": band - 1}, device_id_type=MESH,
         )
 
-    @pl.when(band < n_lat - 1)
-    def _():
-        for c in range(chunks):
+    for c in range(chunks):
+        if c:
+            spread_rows(c)
+
+        @pl.when(band < n_lat - 1)
+        def _():
             upward(c).start()
 
-    @pl.when(band > 0)
-    def _():
-        for c in range(chunks):
+        @pl.when(band > 0)
+        def _():
             downward(c).start()
 
     lane = lax.broadcasted_iota(jnp.int32, (8, 128), 1)
@@ -188,9 +220,6 @@
             return jnp.where(has_north, value, 0.0)
         return value
 
-    def position(slot):
-        return lax.rem(slot, rows), pl.ds(pl.multiple_of((slot // rows) * 8, 8), 8)
-
     def advance_member(c, ml):
         m = c * CHUNK + ml
 
@@ -210,16 +239,7 @@
                 packed[c, q, f // held, pl.ds(ml * held + f % held, 8, stride=8), :] = choose(pieces, q, quarter)
 
     mine, others = pl.ds(pl.multiple_of(me * 8, 8), 8), pl.ds(0, (n_mem - 1) * 8)
-    my_q, my_rows = position(me)
-
-    def peer_of(i):
-        step, kind = i // 4, lax.rem(i, 4)
-        odd = lax.rem(step, 2)
-        dy = n_mem // 8 + (step // 2) * (1 - odd) - ((step + 1) // 2) * odd
-        y = lax.rem(me // 4 + dy, n_mem // 4)
-        x = lax.rem(lax.rem(me, 4) // 2 + 1 - kind // 2, 2)
-        core = lax.rem(lax.rem(me, 2) + 1 - lax.rem(kind, 2), 2)
-        return y * 4 + x * 2 + core
+    my_q, my_rows = me - 4 * my_y, pl.ds(pl.multiple_of(my_y * 8, 8), 8)
 
     def chunk_step(c, _):
         @pl.when(has_south)
@@ -233,22 +253,20 @@
         for ml in range(CHUNK):
             advance_member(c, ml)
 
-        def send(i, _):
-            peer = peer_of(i)
-            q, place = position(peer)
+        for y, q in peers:
             pltpu.make_async_remote_copy(
-                src_ref=packed.at[c, q, :, place], dst_ref=gathered.at[c, :, mine],
+                src_ref=packed.at[c, q, :, pl.ds(pl.multiple_of(y * 8, 8), 8)], dst_ref=gathered.at[c, :, mine],
                 send_sem=send_a.at[c], recv_sem=recv_a.at[c],
-                device_id={"mem": peer}, device_id_type=MESH,
+                device_id={"mem": 4 * y + q}, device_id_type=MESH,
             ).start()
-            return 0
-
-        lax.fori_loop(0, n_mem - 1, send, 0)
+
         gathered[c, :, mine] = packed[c, my_q, :, my_rows]
         return 0
 
     lax.fori_loop(0, chunks, chunk_step, 0)
 
+    for load in small:
+        load.wait()
     nobs = values_ref.shape[1]
     eye = diagonal_of(nobs)
     cells = fields * 128
@@ -303,17 +321,14 @@
         for f in range(fields):
             fresh[c, f // held, pl.ds(f % held, size, stride=held), :] = updated[:, f * 128 : (f + 1) * 128]
 
-        def send_back(i, _):
-            peer = peer_of(i)
-            place = pl.ds(pl.multiple_of(peer * 8, 8), 8)
+        for y, q in peers:
+            place = pl.ds(pl.multiple_of((4 * y + q) * 8, 8), 8)
             pltpu.make_async_remote_copy(
                 src_ref=fresh.at[c, :, place], dst_ref=o_ref.at[c, my_q, :, my_rows],
                 send_sem=send_b.at[c], recv_sem=recv_b.at[c],
-                device_id={"mem": peer}, device_id_type=MESH,
+                device_id={"mem": 4 * y + q}, device_id_type=MESH,
             ).start()
-            return 0
-
-        lax.fori_loop(0, n_mem - 1, send_back, 0)
+
     own = pltpu.make_async_copy(fresh.at[:, :, mine], o_ref.at[:, my_q, :, my_rows], own_b)
     own.start()
 
@@ -336,23 +351,30 @@
         pltpu.make_async_copy(fresh.at[c, :, others], fresh.at[c, :, others], recv_b.at[c]).wait()
 
 
-def unpack_kernel(back_ref, o_ref):
-    rows, spans = back_ref.shape[1], back_ref.shape[2]
+def unpack_kernel(back_ref, o_hbm, o_ref, out_sem):
+    chunks, rows, spans = back_ref.shape[:3]
     fields = o_ref.shape[1]
     held = fields // spans
     quarter = lax.broadcasted_iota(jnp.int32, (8, 128), 1) // 32
-    for ml in range(CHUNK):
-        for f in range(fields):
-            pieces = [back_ref[0, q, f // held, pl.ds(ml * held + f % held, 8, stride=8), :] for q in range(rows)]
-            for r in range(rows):
-                o_ref[ml, f, pl.ds(r, 8, stride=rows), :] = choose(pieces, r, quarter)
+    stores = []
+    for c in range(chunks):
+        for ml in range(CHUNK):
+            for f in range(fields):
+                pieces = [back_ref[c, q, f // held, pl.ds(ml * held + f % held, 8, stride=8), :] for q in range(rows)]
+                for r in range(rows):
+                    o_ref[c * CHUNK + ml, f, pl.ds(r, 8, stride=rows), :] = choose(pieces, r, quarter)
+        part = pl.ds(c * CHUNK, CHUNK)
+        stores.append(pltpu.make_async_copy(o_ref.at[part], o_hbm.at[part], out_sem.at[c]))
+        stores[-1].start()
+    for store in stores:
+        store.wait()
 
 
 def per_device(ensemble, obs_value, obs_var, obs_cell, obs_loop, obs_count):
     members, fields, rows, width = ensemble.shape
     n_mem = lax.axis_size("mem")
     f32 = jnp.float32
-    vmem = pl.BlockSpec(memory_space=pltpu.VMEM)
+    nobs = obs_value.shape[2]
     blocks = width // 128
     chunks = members // CHUNK
     spans = fields * CHUNK // 8
@@ -363,10 +385,16 @@
     )
     back = pl.pallas_call(
         kernel,
-        out_shape=jax.ShapeDtypeStruct((chunks, rows, spans, 64, 128), f32),
-        in_specs=[vmem] * 6,
-        out_specs=pl.BlockSpec(memory_space=pl.ANY),
+        out_shape=pltpu.VMEM((chunks, rows, spans, 64, 128), f32),
+        in_specs=[pl.BlockSpec(memory_space=pl.ANY)] * 6,
+        out_specs=pl.BlockSpec(memory_space=pltpu.VMEM),
         scratch_shapes=[
+            pltpu.VMEM(view.shape, f32),
+            pltpu.VMEM((1, nobs), f32),
+            pltpu.VMEM((1, nobs), f32),
+            pltpu.VMEM((1, nobs), jnp.int32),
+            pltpu.VMEM((1, nobs), jnp.int32),
+            pltpu.VMEM((1, 1), jnp.int32),
             pltpu.VMEM((members, rows + 2 * HALO, fields, 8, 128), f32),
             pltpu.VMEM((rows + 4, fields, 8, 128), f32),
             pltpu.VMEM((rows + 2, fields, 8, 128), f32),
@@ -381,6 +409,8 @@
             pltpu.SemaphoreType.DMA((chunks,)),
             pltpu.SemaphoreType.DMA((chunks,)),
             pltpu.SemaphoreType.DMA,
+            pltpu.SemaphoreType.DMA((chunks,)),
+            pltpu.SemaphoreType.DMA((5,)),
         ],
         compiler_params=pltpu.CompilerParams(collective_id=0, has_side_effects=True),
     )(
@@ -388,11 +418,11 @@
     )
     out = pl.pallas_call(
         unpack_kernel,
-        grid=(chunks,),
         out_shape=jax.ShapeDtypeStruct(view.shape, f32),
-        in_specs=[pl.BlockSpec((1, rows, spans, 64, 128), lambda c: (c, 0, 0, 0, 0))],
-        out_specs=pl.BlockSpec((CHUNK, fields, blocks * rows, 128), lambda c: (c, 0, 0, 0)),
-    )(back)
+        in_specs=[pl.BlockSpec(memory_space=pltpu.VMEM)],
+        out_specs=pl.BlockSpec(memory_space=pl.ANY),
+        scratch_shapes=[pltpu.VMEM(view.shape, f32), pltpu.SemaphoreType.DMA((chunks,))],
+    )(pltpu.with_memory_space_constraint(back, pltpu.VMEM))
     return (
         out.reshape(members, fields, blocks, rows, 128)
         .transpose(0, 1, 3, 2, 4)

time: 64.9 us -> 60.7 us (0.935)
  Pallas kernels: 64 us -> 59.9 us
    pallas_call x2, Pallas kernels: 64 us -> 59.9 us  [the longest x1 58.7 us: per_device(): pl.pallas_call(kernel, out_shape=pltpu.VMEM((chunks, rows, spans, 64, 128...]
where the time goes in v4:
time: 60.7 us; the launch traced here: 60.5 us
  Pallas kernels  59.9 us (99%)
  between operations  0.66 us (1%)
    pallas_call x1, Pallas kernels, per_device(): pl.pallas_call(kernel, out_shape=pltpu.VMEM((chunks, rows, spans, 64, 128...  58.7 us

profile of v4, /device:TPU:3, one launch (start us, length us, event | category | flops | bytes accessed | tf_op | source)
XLA Modules:
  0.0 60.5 jit_solution(16629515480986902520)
XLA Ops:
  0.7 58.7 %shard_map.64.back_ref = f32[4,4,1,64,128]{4,3,2,1,0:T(8,128)S(1)} custom-call(f32[8,4,32,128]{3,2,1,0:T(8,128)} %bitcast.14, f32[1,16]{1,0:T(1,128)} %bitcast.15, f32[1,16]{1,0:T(1,128)} %bitcast.16, s32[1,16]{1,0:T(1,128)} %bitcast.17, s32[1,16]{1,0:T(1,128)} %bitcast.18, s32[1,1]{1,0:T(1,128)S(6)} %copy.9.count_hbm), custom_call_target="tpu_custom_call" | custom-call | tf_op jit(solution)/shard_map/pallas_call | solution.py:386
  59.4 1.2 %shard_map.65 = f32[8,4,32,128]{3,2,1,0:T(8,128)} custom-call(f32[4,4,1,64,128]{4,3,2,1,0:T(8,128)S(1)} %shard_map.64.back_ref), custom_call_target="tpu_custom_call" | custom-call | tf_op jit(solution)/shard_map/pallas_call | solution.py:419

commit v5 on v4

--- a/solution.py
+++ b/solution.py
@@ -86,8 +86,8 @@
 
 def kernel(
     x_hbm, values_hbm, variance_hbm, cell_hbm, loop_hbm, count_hbm, o_ref,
-    x_ref, values_ref, variance_ref, cell_ref, loop_ref, count_ref, wide, mid, mid2, packed, gathered, fresh, centred,
-    halo_send, halo_recv, send_a, recv_a, send_b, recv_b, own_b, load_x, load_small,
+    x_ref, values_ref, variance_ref, cell_ref, loop_ref, count_ref, wide, mid, mid2, packed, gathered, fresh, centred, back,
+    halo_send, halo_recv, send_a, recv_a, send_b, recv_b, load_x, load_small,
 ):
     n_mem, n_lat = lax.axis_size("mem"), lax.axis_size("lat")
     me, band = lax.axis_index("mem"), lax.axis_index("lat")
@@ -321,16 +321,14 @@
         for f in range(fields):
             fresh[c, f // held, pl.ds(f % held, size, stride=held), :] = updated[:, f * 128 : (f + 1) * 128]
 
-        for y, q in peers:
-            place = pl.ds(pl.multiple_of((4 * y + q) * 8, 8), 8)
-            pltpu.make_async_remote_copy(
-                src_ref=fresh.at[c, :, place], dst_ref=o_ref.at[c, my_q, :, my_rows],
-                send_sem=send_b.at[c], recv_sem=recv_b.at[c],
-                device_id={"mem": 4 * y + q}, device_id_type=MESH,
-            ).start()
-
-    own = pltpu.make_async_copy(fresh.at[:, :, mine], o_ref.at[:, my_q, :, my_rows], own_b)
-    own.start()
+    for y, q in peers:
+        place = pl.ds(pl.multiple_of((4 * y + q) * 8, 8), 8)
+        pltpu.make_async_remote_copy(
+            src_ref=fresh.at[:, :, place], dst_ref=back.at[:, my_q, :, my_rows],
+            send_sem=send_b.at[0], recv_sem=recv_b.at[0],
+            device_id={"mem": 4 * y + q}, device_id_type=MESH,
+        ).start()
+    back[:, my_q, :, my_rows] = fresh[:, :, mine]
 
     for c in range(chunks):
         pltpu.make_async_copy(gathered.at[c, :, others], gathered.at[c, :, others], send_a.at[c]).wait()
@@ -345,29 +343,15 @@
         for c in range(chunks):
             downward(c).wait_send()
 
-    own.wait()
-    for c in range(chunks):
-        pltpu.make_async_copy(fresh.at[c, :, others], fresh.at[c, :, others], send_b.at[c]).wait()
-        pltpu.make_async_copy(fresh.at[c, :, others], fresh.at[c, :, others], recv_b.at[c]).wait()
-
-
-def unpack_kernel(back_ref, o_hbm, o_ref, out_sem):
-    chunks, rows, spans = back_ref.shape[:3]
-    fields = o_ref.shape[1]
-    held = fields // spans
-    quarter = lax.broadcasted_iota(jnp.int32, (8, 128), 1) // 32
-    stores = []
+    pltpu.make_async_copy(fresh.at[:, :, others], fresh.at[:, :, others], recv_b.at[0]).wait()
     for c in range(chunks):
         for ml in range(CHUNK):
             for f in range(fields):
-                pieces = [back_ref[c, q, f // held, pl.ds(ml * held + f % held, 8, stride=8), :] for q in range(rows)]
+                pieces = [back[c, q, f // held, pl.ds(ml * held + f % held, 8, stride=8), :] for q in range(rows)]
                 for r in range(rows):
                     o_ref[c * CHUNK + ml, f, pl.ds(r, 8, stride=rows), :] = choose(pieces, r, quarter)
-        part = pl.ds(c * CHUNK, CHUNK)
-        stores.append(pltpu.make_async_copy(o_ref.at[part], o_hbm.at[part], out_sem.at[c]))
-        stores[-1].start()
-    for store in stores:
-        store.wait()
+
+    pltpu.make_async_copy(fresh.at[:, :, others], fresh.at[:, :, others], send_b.at[0]).wait()
 
 
 def per_device(ensemble, obs_value, obs_var, obs_cell, obs_loop, obs_count):
@@ -383,9 +367,9 @@
         .transpose(0, 1, 3, 2, 4)
         .reshape(members, fields, blocks * rows, 128)
     )
-    back = pl.pallas_call(
+    out = pl.pallas_call(
         kernel,
-        out_shape=pltpu.VMEM((chunks, rows, spans, 64, 128), f32),
+        out_shape=pltpu.VMEM(view.shape, f32),
         in_specs=[pl.BlockSpec(memory_space=pl.ANY)] * 6,
         out_specs=pl.BlockSpec(memory_space=pltpu.VMEM),
         scratch_shapes=[
@@ -402,13 +386,13 @@
             pltpu.VMEM((chunks, spans, n_mem * 8, 128), f32),
             pltpu.VMEM((chunks, spans, n_mem * 8, 128), f32),
             pltpu.VMEM((chunks, n_mem * CHUNK, fields * 128), f32),
+            pltpu.VMEM((chunks, rows, spans, 64, 128), f32),
             pltpu.SemaphoreType.DMA((2, chunks)),
             pltpu.SemaphoreType.DMA((2, chunks)),
             pltpu.SemaphoreType.DMA((chunks,)),
             pltpu.SemaphoreType.DMA((chunks,)),
             pltpu.SemaphoreType.DMA((chunks,)),
             pltpu.SemaphoreType.DMA((chunks,)),
-            pltpu.SemaphoreType.DMA,
             pltpu.SemaphoreType.DMA((chunks,)),
             pltpu.SemaphoreType.DMA((5,)),
         ],
@@ -416,13 +400,6 @@
     )(
         view, obs_value[0], obs_var[0], obs_cell[0], obs_loop[0], obs_count,
     )
-    out = pl.pallas_call(
-        unpack_kernel,
-        out_shape=jax.ShapeDtypeStruct(view.shape, f32),
-        in_specs=[pl.BlockSpec(memory_space=pltpu.VMEM)],
-        out_specs=pl.BlockSpec(memory_space=pl.ANY),
-        scratch_shapes=[pltpu.VMEM(view.shape, f32), pltpu.SemaphoreType.DMA((chunks,))],
-    )(pltpu.with_memory_space_constraint(back, pltpu.VMEM))
     return (
         out.reshape(members, fields, blocks, rows, 128)
         .transpose(0, 1, 3, 2, 4)

time: 60.7 us -> 60.4 us (level)
  Pallas kernels: 59.9 us -> 58.5 us
  local copies, waits for them, and re-layouts: 0 us -> 0.8 us
    pallas_call x2 -> x1, Pallas kernels: 59.9 us -> 58.5 us  [per_device(): pl.pallas_call(kernel, out_shape=pltpu.VMEM(view.shape, f32), in_specs=[p...]
    unnamed x0 -> x1, local copies, waits for them, and re-layouts: none -> 0.8 us
where the time goes in v5:
time: 60.4 us; the launch traced here: 60 us
  Pallas kernels  58.5 us (97%)
  local copies, waits for them, and re-layouts  0.8 us (1%)
  between operations  0.66 us (1%)
    pallas_call x1, Pallas kernels, per_device(): pl.pallas_call(kernel, out_shape=pltpu.VMEM(view.shape, f32), in_specs=[p...  58.5 us

profile of v5, /device:TPU:3, one launch (start us, length us, event | category | flops | bytes accessed | tf_op | source)
XLA Modules:
  0.0 60.0 jit_solution(10025924036006632043)
XLA Ops:
  0.7 58.5 %shard_map.64 = f32[8,4,32,128]{3,2,1,0:T(8,128)S(1)} custom-call(f32[8,4,32,128]{3,2,1,0:T(8,128)} %bitcast.15, f32[1,16]{1,0:T(1,128)} %bitcast.16, f32[1,16]{1,0:T(1,128)} %bitcast.17, s32[1,16]{1,0:T(1,128)} %bitcast.18, s32[1,16]{1,0:T(1,128)} %bitcast.19, s32[1,1]{1,0:T(1,128)S(6)} %copy.11.count_hbm), custom_call_target="tpu_custom_call" | custom-call | tf_op jit(solution)/shard_map/pallas_call | solution.py:370
  59.2 0.8 %copy.10 = f32[8,4,4,1024]{3,2,1,0:T(4,128)} copy(f32[8,4,4,1024]{3,2,1,0:T(4,128)S(1)} %bitcast.14) | data formatting | bytes 1048576

commit v6 on v5

--- a/solution.py
+++ b/solution.py
@@ -9,7 +9,7 @@
 NSI = 5
 DT = 0.15
 VISC = 0.1
-CHUNK = 2
+CHUNK = 1
 HALO = 3
 
 
@@ -96,6 +96,7 @@
     chunks = members // CHUNK
     spans = packed.shape[2]
     held = fields // spans
+    tile = CHUNK * held
 
     loads = [
         pltpu.make_async_copy(
@@ -236,10 +237,10 @@
         for f in range(fields):
             pieces = [result[r, f] for r in range(rows)]
             for q in range(rows):
-                packed[c, q, f // held, pl.ds(ml * held + f % held, 8, stride=8), :] = choose(pieces, q, quarter)
-
-    mine, others = pl.ds(pl.multiple_of(me * 8, 8), 8), pl.ds(0, (n_mem - 1) * 8)
-    my_q, my_rows = me - 4 * my_y, pl.ds(pl.multiple_of(my_y * 8, 8), 8)
+                packed[c, q, f // held, pl.ds(ml * held + f % held, 8, stride=tile), :] = choose(pieces, q, quarter)
+
+    mine, others = pl.ds(pl.multiple_of(me * tile, tile), tile), pl.ds(0, (n_mem - 1) * tile)
+    my_q, my_rows = me - 4 * my_y, pl.ds(pl.multiple_of(my_y * tile, tile), tile)
 
     def chunk_step(c, _):
         @pl.when(has_south)
@@ -255,7 +256,7 @@
 
         for y, q in peers:
             pltpu.make_async_remote_copy(
-                src_ref=packed.at[c, q, :, pl.ds(pl.multiple_of(y * 8, 8), 8)], dst_ref=gathered.at[c, :, mine],
+                src_ref=packed.at[c, q, :, pl.ds(pl.multiple_of(y * tile, tile), tile)], dst_ref=gathered.at[c, :, mine],
                 send_sem=send_a.at[c], recv_sem=recv_a.at[c],
                 device_id={"mem": 4 * y + q}, device_id_type=MESH,
             ).start()
@@ -322,7 +323,7 @@
             fresh[c, f // held, pl.ds(f % held, size, stride=held), :] = updated[:, f * 128 : (f + 1) * 128]
 
     for y, q in peers:
-        place = pl.ds(pl.multiple_of((4 * y + q) * 8, 8), 8)
+        place = pl.ds(pl.multiple_of((4 * y + q) * tile, tile), tile)
         pltpu.make_async_remote_copy(
             src_ref=fresh.at[:, :, place], dst_ref=back.at[:, my_q, :, my_rows],
             send_sem=send_b.at[0], recv_sem=recv_b.at[0],
@@ -347,7 +348,7 @@
     for c in range(chunks):
         for ml in range(CHUNK):
             for f in range(fields):
-                pieces = [back[c, q, f // held, pl.ds(ml * held + f % held, 8, stride=8), :] for q in range(rows)]
+                pieces = [back[c, q, f // held, pl.ds(ml * held + f % held, 8, stride=tile), :] for q in range(rows)]
                 for r in range(rows):
                     o_ref[c * CHUNK + ml, f, pl.ds(r, 8, stride=rows), :] = choose(pieces, r, quarter)
 
@@ -361,7 +362,8 @@
     nobs = obs_value.shape[2]
     blocks = width // 128
     chunks = members // CHUNK
-    spans = fields * CHUNK // 8
+    spans = max(1, fields * CHUNK // 8)
+    tile = CHUNK * fields // spans
     view = (
         ensemble.reshape(members, fields, rows, blocks, 128)
         .transpose(0, 1, 3, 2, 4)
@@ -382,11 +384,11 @@
             pltpu.VMEM((members, rows + 2 * HALO, fields, 8, 128), f32),
             pltpu.VMEM((rows + 4, fields, 8, 128), f32),
             pltpu.VMEM((rows + 2, fields, 8, 128), f32),
-            pltpu.VMEM((chunks, rows, spans, 64, 128), f32),
-            pltpu.VMEM((chunks, spans, n_mem * 8, 128), f32),
-            pltpu.VMEM((chunks, spans, n_mem * 8, 128), f32),
+            pltpu.VMEM((chunks, rows, spans, 8 * tile, 128), f32),
+            pltpu.VMEM((chunks, spans, n_mem * tile, 128), f32),
+            pltpu.VMEM((chunks, spans, n_mem * tile, 128), f32),
             pltpu.VMEM((chunks, n_mem * CHUNK, fields * 128), f32),
-            pltpu.VMEM((chunks, rows, spans, 64, 128), f32),
+            pltpu.VMEM((chunks, rows, spans, 8 * tile, 128), f32),
             pltpu.SemaphoreType.DMA((2, chunks)),
             pltpu.SemaphoreType.DMA((2, chunks)),
             pltpu.SemaphoreType.DMA((chunks,)),

time: 60.4 us -> 59 us (0.977)
  Pallas kernels: 58.5 us -> 57.1 us
    pallas_call x1, Pallas kernels: 58.5 us -> 57.1 us  [per_device(): pl.pallas_call(kernel, out_shape=pltpu.VMEM(view.shape, f32), in_specs=[p...]
where the time goes in v6:
time: 59 us; the launch traced here: 58.5 us
  Pallas kernels  57.1 us (97%)
  local copies, waits for them, and re-layouts  0.8 us (1%)
  between operations  0.66 us (1%)
    pallas_call x1, Pallas kernels, per_device(): pl.pallas_call(kernel, out_shape=pltpu.VMEM(view.shape, f32), in_specs=[p...  57.1 us

profile of v6, /device:TPU:3, one launch (start us, length us, event | category | flops | bytes accessed | tf_op | source)
XLA Modules:
  0.0 58.5 jit_solution(90598472637644313)
XLA Ops:
  0.7 57.1 %shard_map.64 = f32[8,4,32,128]{3,2,1,0:T(8,128)S(1)} custom-call(f32[8,4,32,128]{3,2,1,0:T(8,128)} %bitcast.15, f32[1,16]{1,0:T(1,128)} %bitcast.16, f32[1,16]{1,0:T(1,128)} %bitcast.17, s32[1,16]{1,0:T(1,128)} %bitcast.18, s32[1,16]{1,0:T(1,128)} %bitcast.19, s32[1,1]{1,0:T(1,128)S(6)} %copy.11.count_hbm), custom_call_target="tpu_custom_call" | custom-call | tf_op jit(solution)/shard_map/pallas_call | solution.py:372
  57.7 0.8 %copy.10 = f32[8,4,4,1024]{3,2,1,0:T(4,128)} copy(f32[8,4,4,1024]{3,2,1,0:T(4,128)S(1)} %bitcast.14) | data formatting | bytes 1048576
